TPU v7x, 256 devices: a whole 4x4x8 slice. The times are simulated.
256 devices in a mesh: site: 16 (over z_lo, x), phonon: 16 (over y, z_hi, core).
Axes of the slice: x: 4, y: 4, z: 8 (z_hi: 2, z_lo: 4; z = z_hi * 4 + z_lo), core: 2. Of those that a mesh axis runs over, the one named last changes fastest.
Arguments:
- state: float32 [16384, 2048], P('site', 'phonon'), may hold values from -4.5 to 6.5
- operators: bfloat16 [4, 1024, 1024], replicated, may hold values from -0.1875 to 0.1875
- op_mask: int32 [4, 8, 8], replicated, may hold values 0 or 1
- site_bits: int32 [4], replicated, may hold values from 0 to 3, each once
- field: float32 [4], replicated, may hold values from 0.25 to 1
- site_coupling: float32 [14], replicated, may hold values from 0.1 to 0.6
- mode_coupling: float32 [64], replicated, may hold values from 0.2 to 1
Outputs:
- chebyshev_last: float32 [16384, 2048], P('site', 'phonon')
- chebyshev_prev: float32 [16384, 2048], P('site', 'phonon')
- moments: float32 [3], replicated
Inputs may be any that keep to these rules, and one draw needn't show every extreme that they name: `site_bits`: each of 0 to 3 exactly once.
All inputs are finite; a program needn't handle non-finite values.
Results may differ from a plain program's by a relative error of at most 0.0011.
The roundings to bfloat16 on the way count: a program that leaves them out, or rounds other values in their place, can miss the bound.
Values sent between devices are 32-bit elements; how exact they have to be, the bound alone decides.
A program may use at most 64 MiB of HBM per device.

v0:
```python
import jax
import jax.numpy as jnp
from jax import lax
from jax.sharding import PartitionSpec as P

LBITS = 10
MODES = 64
LEV_DEV = 2
STEPS = 3


epsilon = 1e-06


def extended_2(block, sides, width):
    for axis, dim in sides:
        count = lax.axis_size(axis)
        forward = [(i, i + 1) for i in range(count - 1)]
        backward = [(target, source) for source, target in forward]
        low = lax.ppermute(
            lax.slice_in_dim(block, block.shape[dim] - width, None, axis=dim), axis, forward
        )
        high = lax.ppermute(lax.slice_in_dim(block, 0, width, axis=dim), axis, backward)
        block = jnp.concatenate([low, block, high], axis=dim)
    return block


def partner(value, axis, bit):
    mask = 2**bit
    pairs = [(source, source ^ mask) for source in range(lax.axis_size(axis))]
    return lax.ppermute(value, axis, pairs)


def shards(state, operators, op_mask, site_bits, field, site_coupling, mode_coupling):
    site_count = lax.axis_size("site")
    phonon_count = lax.axis_size("phonon")
    bit_count = site_count.bit_length() - 1
    rows_here = state.shape[0]
    columns_here = state.shape[1]
    block_edge = rows_here // op_mask.shape[1]
    expanded = jnp.repeat(jnp.repeat(op_mask, block_edge, axis=1), block_edge, axis=2)
    masked = jnp.where(expanded > 0, operators, jnp.zeros((), jnp.bfloat16))
    entries = jnp.float32(rows_here * columns_here * site_count * phonon_count)
    level_total = jnp.sqrt(jnp.float32(LEV_DEV * phonon_count))
    device = lax.axis_index("site")
    inside = lax.iota(jnp.int32, rows_here)
    weight_rows = jnp.zeros((rows_here,), jnp.float32)
    for position in range(bit_count):
        weight_rows = weight_rows + site_coupling[site_bits[position]] * (
            device >> position & 1
        ).astype(jnp.float32)
    for local_bit in range(LBITS):
        weight_rows = weight_rows + site_coupling[bit_count + local_bit] * (
            inside >> local_bit & 1
        ).astype(jnp.float32)
    levels = (
        lax.axis_index("phonon") * LEV_DEV + lax.iota(jnp.int32, columns_here) // MODES
    ).astype(jnp.float32)
    lower_weight = jnp.sqrt(levels)
    upper_weight = jnp.sqrt(levels + 1.0)
    mode_weight = jnp.tile(mode_coupling, columns_here // MODES) / level_total
    start_squares = lax.psum(jnp.sum(state * state), ("site", "phonon"))
    initial = state / jnp.sqrt(start_squares / entries + epsilon)
    previous = initial
    current = initial
    scale_prev = jnp.float32(1.0)
    moments = []
    for iteration in range(STEPS):
        extended = extended_2(current, (("phonon", 1),), MODES)
        lower_part = extended[:, :columns_here]
        upper_part = extended[:, 2 * MODES :]
        summed = weight_rows[:, None] * (
            mode_weight * (lower_weight * lower_part + upper_weight * upper_part)
        )
        for operate_position in range(bit_count):
            chosen = site_bits[operate_position]
            flipped = partner(current, "site", operate_position)
            product = jnp.dot(
                masked[chosen], flipped.astype(jnp.bfloat16), preferred_element_type=jnp.float32
            )
            summed = summed + (field[chosen] * flipped + product)
        if iteration == 0:
            vector_new = summed
        else:
            vector_new = 2.0 * summed - previous / scale_prev
        squares = lax.psum(jnp.sum(vector_new * vector_new), ("site", "phonon"))
        scale_now = jnp.sqrt(squares / entries + epsilon)
        updated = vector_new / scale_now
        moment = lax.psum(jnp.sum(initial * updated), ("site", "phonon")) / entries
        moments.append(moment)
        previous = current
        current = updated
        scale_prev = scale_now
    return (current, previous, jnp.stack(moments))


def solution(mesh):
    in_specs = (P("site", "phonon"), P(), P(), P(), P(), P(), P())
    out_specs = (P("site", "phonon"), P("site", "phonon"), P())
    return jax.shard_map(shards, mesh=mesh, in_specs=in_specs, out_specs=out_specs, check_vma=False)
```

profile of v0, /device:TPU:1, one launch (start us, length us, event | category | flops | bytes accessed | tf_op | source)
XLA Modules:
  0.0 575.4 jit_solution(10038324264010746396)
XLA Ops:
  0.6 1.8 multiply_reduce_fusion.6
  2.4 1.2 copy.10
  3.7 81.4 %psum.49 = f32[]{:T(128)} all-reduce(f32[]{:T(128)} %multiply_reduce_fusion.6), channel_id=1, replica_groups=mesh['site'=16,'phonon'=16] {'site','phonon'}, use_global_device_ids=true, to_apply=%region_1.2 | all-reduce | flops 1 | bytes 8 | tf_op jit(solution)/shard_map/psum | solution.py:62
  85.7 0.1 broadcast_divide_fusion.3
  85.8 0.8 collective-permute-start.4
  86.6 1.2 collective-permute-start.3
  87.7 1.2 collective-permute-start.5
  88.9 0.8 fusion.108
  89.7 5.6 collective-permute-start
  95.4 1.5 fusion.111
  102.0 0.7 broadcast_compare_fusion
  102.7 0.1 broadcast_in_dim.8
  102.8 14.8 %broadcast_in_dim.9 = pred[4,1024,8,128]{3,2,1,0:T(8,128)(4,1)} broadcast(pred[4,1024,8]{2,1,0:T(8,128)(4,1)S(1)} %bitcast.68), dimensions={0,1,2} | broadcast | bytes 4227072 | tf_op jit(solution)/shard_map/broadcast_in_dim | solution.py:41
  117.6 12.0 %gt.17 = pred[4,1024,1024]{2,1,0:T(8,128)(4,1)} reshape(pred[4,1024,8,128]{3,2,1,0:T(8,128)(4,1)} %broadcast_in_dim.9) | data formatting | bytes 8388608 | tf_op jit(solution)/shard_map/gt | solution.py:42
  132.2 8.7 %broadcast_select_fusion = bf16[4,1024,1024]{2,1,0:T(8,128)(2,1)} fusion(pred[4,1024,1024]{2,1,0:T(8,128)(4,1)} %gt.17, bf16[4,1024,1024]{2,1,0:T(8,128)(2,1)} %param.8), kind=kLoop, calls=%fused_computation | loop fusion | flops 4194304 | bytes 20971520 | tf_op jit(solution)/shard_map/jit(_where)/select_n | solution.py:42
  140.9 0.7 fusion.109
  144.2 6.2 %multiply_add_fusion = f32[1024]{0:T(1024)S(1)} fusion(f32[]{:T(128)} %bitcast.17, f32[]{:T(128)} %bitcast.16, f32[]{:T(128)} %bitcast.15, f32[]{:T(128)} %bitcast.14, f32[]{:T(128)} %bitcast.13, f32[]{:T(128)} %bitcast.12, f32[]{:T(128)} %bitcast.11, f32[]{:T(128)} %bitcast.10, f32[]{:T(128)} %bitcast.9, f32[]{:T(128)} %bitcast.8, f32[]{:T(128)S(6)} %add.276), kind=kLoop, calls=%fused_computation.98 | loop fusion | flops 51200 | bytes 4140 | tf_op jit(solution)/shard_map/add | solution.py:53
  155.5 0.1 div.75
  155.6 0.7 fusion.110
  156.3 1.9 collective-permute-start.1
  158.2 2.4 fusion.10
  160.6 2.4 fusion.16
  163.1 2.4 fusion.22
  165.5 2.7 collective-permute-done.1
  168.2 0.8 copy-done.1
  169.0 6.1 %multiply_reduce_fusion.5 = (f32[]{:T(128)}, f32[1024,128]{0,1:T(8,128)S(1)}) fusion(f32[1024,128]{0,1:T(8,128)} %copy-done.1, bf16[4,1024,1024]{2,1,0:T(8,128)(2,1)} %broadcast_select_fusion, s32[]{:T(128)S(6)} %select_n.69, f32[]{:T(128)} %bitcast.25, f32[1024,128]{0,1:T(8,128)S(1)} %fusion.10, f32[1024,128]{0,1:T(8,128)S(1)} %collective-permute-done.4, ...), kind=kOutput, calls=%fused_computation.79 | convolution fusion | flops 271319040 | bytes 7872008 | tf_op jit(solution)/shard_map/dot_general | solution.py:78
  175.0 77.3 %psum.50 = f32[]{:T(128)} all-reduce(f32[]{:T(128)} %get-tuple-element.41), channel_id=1, replica_groups=mesh['site'=16,'phonon'=16] {'site','phonon'}, use_global_device_ids=true, to_apply=%region_3.4 | all-reduce | flops 1 | bytes 8 | tf_op jit(solution)/shard_map/psum | solution.py:86
  253.1 0.1 collective-permute-start.8
  253.2 2.0 collective-permute-start.9
  255.3 1.7 collective-permute-start.10
  256.9 0.7 fusion.107
  257.7 1.0 collective-permute-start.11
  258.7 5.8 %collective-permute-start.6 = (f32[1024,64]{0,1:T(8,128)}, f32[1024,64]{0,1:T(8,128)S(1)}, u32[]{:S(2)}, u32[]{:S(2)}) collective-permute-start(f32[1024,64]{0,1:T(8,128)} %get-tuple-element.15), channel_id=1, source_target_pairs={{0,1},{1,2},{2,3},{3,4},{4,5},{5,6},{6,7},{7,8},{8,9},{9,10},{10,1... | collective-permute-start | bytes 786440 | tf_op jit(solution)/shard_map/ppermute | solution.py:20
  264.5 1.7 collective-permute-done.8
  266.1 4.6 collective-permute-start.7
  270.7 2.4 fusion.20
  273.2 4.7 collective-permute-done.9
  277.9 2.4 fusion.14
  280.3 2.6 fusion.8
  282.9 4.8 collective-permute-done.6
  287.7 4.2 collective-permute-done.7
  292.0 6.3 %multiply_reduce_fusion.4 = (f32[]{:T(128)}, f32[1024,128]{0,1:T(8,128)S(1)}) fusion(f32[1024,128]{0,1:T(8,128)S(1)} %copy.10, f32[]{:T(128)S(6)} %multiply.22, f32[1024,128]{0,1:T(8,128)} %collective-permute-done.11, bf16[4,1024,1024]{2,1,0:T(8,128)(2,1)} %broadcast_select_fusion, s32[]{:T(128)S(6)} %select_n.69, f32[]{:T(128)} %bitcast.25, ...), kind=kOutput, calls=%fused_computation.78 | convolution fusion | flops 271712256 | bytes 8396300 | tf_op jit(solution)/shard_map/dot_general | solution.py:78
  298.3 75.0 %psum.51 = f32[]{:T(128)} all-reduce(f32[]{:T(128)} %get-tuple-element.43), channel_id=1, replica_groups=mesh['site'=16,'phonon'=16] {'site','phonon'}, use_global_device_ids=true, to_apply=%region_5.6 | all-reduce | flops 1 | bytes 8 | tf_op jit(solution)/shard_map/psum | solution.py:86
  374.0 0.4 collective-permute-start.14
  374.4 2.4 collective-permute-start.15
  376.8 1.2 collective-permute-start.16
  378.0 0.7 fusion.106
  378.8 1.5 collective-permute-start.17
  380.3 1.0 copy.17
  381.2 5.6 collective-permute-start.12
  386.9 0.1 collective-permute-done.14
  387.0 4.4 collective-permute-start.13
  391.5 2.4 fusion.18
  393.9 5.5 collective-permute-done.15
  399.4 2.4 fusion.12
  401.8 2.5 fusion.6
  404.3 4.3 collective-permute-done.12
  408.6 5.0 collective-permute-done.13
  413.6 7.1 %multiply_reduce_fusion.3 = (f32[]{:T(128)}, f32[1024,128]{0,1:T(8,128)}) fusion(f32[1024,128]{0,1:T(8,128)S(1)} %get-tuple-element.42, f32[]{:T(128)S(6)} %multiply.23, f32[1024,128]{0,1:T(8,128)} %collective-permute-done.17, bf16[4,1024,1024]{2,1,0:T(8,128)(2,1)} %broadcast_select_fusion, s32[]{:T(128)S(6)} %select_n.69, f32[]{:T(128)} %bitcast.25, ...), kind=kOutput, calls=%fused_computation.77 | convolution fusion | flops 271712256 | bytes 8396300 | tf_op jit(solution)/shard_map/dot_general | solution.py:78
  420.7 74.8 %psum.52 = f32[]{:T(128)} all-reduce(f32[]{:T(128)} %get-tuple-element.45), channel_id=1, replica_groups=mesh['site'=16,'phonon'=16] {'site','phonon'}, use_global_device_ids=true, to_apply=%region_7.8 | all-reduce | flops 1 | bytes 8 | tf_op jit(solution)/shard_map/psum | solution.py:86
  496.2 1.9 multiply_reduce_fusion.2
  498.1 73.7 %all-reduce = (f32[]{:T(128)}, f32[]{:T(128)}, f32[]{:T(128)}) all-reduce(f32[]{:T(128)} %get-tuple-element.8, f32[]{:T(128)} %get-tuple-element.7, f32[]{:T(128)} %get-tuple-element.6), channel_id=1, replica_groups=mesh['site'=16,'phonon'=16] {'site','phonon'}, use_global_device_ids=true, to_apply=%region_13.14 | all-reduce | flops 3 | bytes 24 | tf_op jit(solution)/shard_map/psum | solution.py:89
  573.8 1.0 copy.16
  574.8 0.6 pad_maximum_fusion.6
  (24 shorter events, 0.2 us)
Async XLA Ops:
  85.8 70.5 %collective-permute-start.4 = (f32[1024,128]{0,1:T(8,128)S(1)}, f32[1024,128]{0,1:T(8,128)S(1)}, u32[]{:S(2)}, u32[]{:S(2)}) collective-permute-start(f32[1024,128]{0,1:T(8,128)S(1)} %broadcast_divide_fusion.3), channel_id=1, source_target_pairs={{0,64},{16,80},{32,96},{48,112},{64,0},{80,16},{96,32},{112,48},{1... | collective-permute-start | bytes 1572872 | tf_op jit(solution)/shard_map/ppermute | solution.py:31
  86.6 74.1 %collective-permute-start.3 = (f32[1024,128]{0,1:T(8,128)S(1)}, f32[1024,128]{0,1:T(8,128)S(1)}, u32[]{:S(2)}, u32[]{:S(2)}) collective-permute-start(f32[1024,128]{0,1:T(8,128)S(1)} %broadcast_divide_fusion.3), channel_id=1, source_target_pairs={{0,32},{16,48},{32,0},{48,16},{64,96},{80,112},{96,64},{112,80},{1... | collective-permute-start | bytes 1572872 | tf_op jit(solution)/shard_map/ppermute | solution.py:31
  87.7 75.3 %collective-permute-start.2 = (f32[1024,128]{0,1:T(8,128)S(1)}, f32[1024,128]{0,1:T(8,128)S(1)}, u32[]{:S(2)}, u32[]{:S(2)}) collective-permute-start(f32[1024,128]{0,1:T(8,128)S(1)} %broadcast_divide_fusion.3), channel_id=1, source_target_pairs={{0,16},{16,0},{32,48},{48,32},{64,80},{80,64},{96,112},{112,96},{1... | collective-permute-start | bytes 1572872 | tf_op jit(solution)/shard_map/ppermute | solution.py:31
  87.7 80.4 %collective-permute-start.5 = (f32[1024,128]{0,1:T(8,128)S(1)}, f32[1024,128]{0,1:T(8,128)S(1)}, u32[]{:S(2)}, u32[]{:S(2)}) collective-permute-start(f32[1024,128]{0,1:T(8,128)S(1)} %broadcast_divide_fusion.3), channel_id=1, source_target_pairs={{0,128},{16,144},{32,160},{48,176},{64,192},{80,208},{96,224},{112... | collective-permute-start | bytes 1572872 | tf_op jit(solution)/shard_map/ppermute | solution.py:31
  89.7 75.8 %collective-permute-start = (f32[1024,64]{0,1:T(8,128)}, f32[1024,64]{0,1:T(8,128)S(1)}, u32[]{:S(2)}, u32[]{:S(2)}) collective-permute-start(f32[1024,64]{0,1:T(8,128)} %get-tuple-element.17), channel_id=1, source_target_pairs={{0,1},{1,2},{2,3},{3,4},{4,5},{5,6},{6,7},{7,8},{8,9},{9,10},{10,1... | collective-permute-start | bytes 786440 | tf_op jit(solution)/shard_map/ppermute | solution.py:20
  132.2 8.7 %copy-start.4 = (f32[64]{0:T(128)S(1)}, f32[64]{0:T(128)}, u32[]{:S(2)}) copy-start(f32[64]{0:T(128)} %param.13) | copy-start | bytes 772
  132.2 8.7 %copy-start.2 = (f32[14]{0:T(128)S(1)}, f32[14]{0:T(128)}, u32[]{:S(2)}) copy-start(f32[14]{0:T(128)} %param.12) | copy-start | bytes 172
  132.2 23.4 %copy-start.3 = (f32[4]{0:T(128)S(1)}, f32[4]{0:T(128)}, u32[]{:S(2)}) copy-start(f32[4]{0:T(128)} %param.11) | copy-start | bytes 52
  156.3 11.9 %collective-permute-start.1 = (f32[1024,64]{0,1:T(8,128)}, f32[1024,64]{0,1:T(8,128)S(1)}, u32[]{:S(2)}, u32[]{:S(2)}) collective-permute-start(f32[1024,64]{0,1:T(8,128)} %get-tuple-element.18), channel_id=1, source_target_pairs={{1,0},{2,1},{3,2},{4,3},{5,4},{6,5},{7,6},{8,7},{9,8},{10,9},{11,1... | collective-permute-start | bytes 786440 | tf_op jit(solution)/shard_map/ppermute | solution.py:23
  168.2 0.8 copy-start.1
  253.1 13.0 %collective-permute-start.8 = (f32[1024,128]{0,1:T(8,128)S(1)}, f32[1024,128]{0,1:T(8,128)S(1)}, u32[]{:S(2)}, u32[]{:S(2)}) collective-permute-start(f32[1024,128]{0,1:T(8,128)S(1)} %broadcast_divide_fusion.2), channel_id=1, source_target_pairs={{0,16},{16,0},{32,48},{48,32},{64,80},{80,64},{96,112},{112,96},{1... | collective-permute-start | bytes 1572872 | tf_op jit(solution)/shard_map/ppermute | solution.py:31
  253.2 24.6 %collective-permute-start.9 = (f32[1024,128]{0,1:T(8,128)S(1)}, f32[1024,128]{0,1:T(8,128)S(1)}, u32[]{:S(2)}, u32[]{:S(2)}) collective-permute-start(f32[1024,128]{0,1:T(8,128)S(1)} %broadcast_divide_fusion.2), channel_id=1, source_target_pairs={{0,32},{16,48},{32,0},{48,16},{64,96},{80,112},{96,64},{112,80},{1... | collective-permute-start | bytes 1572872 | tf_op jit(solution)/shard_map/ppermute | solution.py:31
  255.3 25.0 %collective-permute-start.10 = (f32[1024,128]{0,1:T(8,128)S(1)}, f32[1024,128]{0,1:T(8,128)S(1)}, u32[]{:S(2)}, u32[]{:S(2)}) collective-permute-start(f32[1024,128]{0,1:T(8,128)S(1)} %broadcast_divide_fusion.2), channel_id=1, source_target_pairs={{0,64},{16,80},{32,96},{48,112},{64,0},{80,16},{96,32},{112,48},{1... | collective-permute-start | bytes 1572872 | tf_op jit(solution)/shard_map/ppermute | solution.py:31
  257.7 34.3 %collective-permute-start.11 = (f32[1024,128]{0,1:T(8,128)S(1)}, f32[1024,128]{0,1:T(8,128)}, u32[]{:S(2)}, u32[]{:S(2)}) collective-permute-start(f32[1024,128]{0,1:T(8,128)S(1)} %broadcast_divide_fusion.2), channel_id=1, source_target_pairs={{0,128},{16,144},{32,160},{48,176},{64,192},{80,208},{96,224},{112... | collective-permute-start | bytes 1572872 | tf_op jit(solution)/shard_map/ppermute | solution.py:31
  258.7 29.1 %collective-permute-start.6 = (f32[1024,64]{0,1:T(8,128)}, f32[1024,64]{0,1:T(8,128)S(1)}, u32[]{:S(2)}, u32[]{:S(2)}) collective-permute-start(f32[1024,64]{0,1:T(8,128)} %get-tuple-element.15), channel_id=1, source_target_pairs={{0,1},{1,2},{2,3},{3,4},{4,5},{5,6},{6,7},{7,8},{8,9},{9,10},{10,1... | collective-permute-start | bytes 786440 | tf_op jit(solution)/shard_map/ppermute | solution.py:20
  266.1 25.9 %collective-permute-start.7 = (f32[1024,64]{0,1:T(8,128)S(1)}, f32[1024,64]{0,1:T(8,128)S(1)}, u32[]{:S(2)}, u32[]{:S(2)}) collective-permute-start(f32[1024,64]{0,1:T(8,128)S(1)} %get-tuple-element.16), channel_id=1, source_target_pairs={{1,0},{2,1},{3,2},{4,3},{5,4},{6,5},{7,6},{8,7},{9,8},{10,9},{11,1... | collective-permute-start | bytes 786440 | tf_op jit(solution)/shard_map/ppermute | solution.py:23
  280.3 11.7 %copy-start = (f32[1024,128]{0,1:T(8,128)}, f32[1024,128]{0,1:T(8,128)S(1)}, u32[]{:S(2)}) copy-start(f32[1024,128]{0,1:T(8,128)S(1)} %collective-permute-done.10) | copy-start | bytes 1572868
  374.0 13.0 %collective-permute-start.14 = (f32[1024,128]{0,1:T(8,128)S(1)}, f32[1024,128]{0,1:T(8,128)S(1)}, u32[]{:S(2)}, u32[]{:S(2)}) collective-permute-start(f32[1024,128]{0,1:T(8,128)S(1)} %broadcast_divide_fusion.1), channel_id=1, source_target_pairs={{0,16},{16,0},{32,48},{48,32},{64,80},{80,64},{96,112},{112,96},{1... | collective-permute-start | bytes 1572872 | tf_op jit(solution)/shard_map/ppermute | solution.py:31
  374.4 25.0 %collective-permute-start.15 = (f32[1024,128]{0,1:T(8,128)S(1)}, f32[1024,128]{0,1:T(8,128)S(1)}, u32[]{:S(2)}, u32[]{:S(2)}) collective-permute-start(f32[1024,128]{0,1:T(8,128)S(1)} %broadcast_divide_fusion.1), channel_id=1, source_target_pairs={{0,32},{16,48},{32,0},{48,16},{64,96},{80,112},{96,64},{112,80},{1... | collective-permute-start | bytes 1572872 | tf_op jit(solution)/shard_map/ppermute | solution.py:31
  376.8 25.0 %collective-permute-start.16 = (f32[1024,128]{0,1:T(8,128)S(1)}, f32[1024,128]{0,1:T(8,128)}, u32[]{:S(2)}, u32[]{:S(2)}) collective-permute-start(f32[1024,128]{0,1:T(8,128)S(1)} %broadcast_divide_fusion.1), channel_id=1, source_target_pairs={{0,64},{16,80},{32,96},{48,112},{64,0},{80,16},{96,32},{112,48},{1... | collective-permute-start | bytes 1572872 | tf_op jit(solution)/shard_map/ppermute | solution.py:31
  378.8 34.8 %collective-permute-start.17 = (f32[1024,128]{0,1:T(8,128)S(1)}, f32[1024,128]{0,1:T(8,128)}, u32[]{:S(2)}, u32[]{:S(2)}) collective-permute-start(f32[1024,128]{0,1:T(8,128)S(1)} %broadcast_divide_fusion.1), channel_id=1, source_target_pairs={{0,128},{16,144},{32,160},{48,176},{64,192},{80,208},{96,224},{112... | collective-permute-start | bytes 1572872 | tf_op jit(solution)/shard_map/ppermute | solution.py:31
  381.2 27.3 %collective-permute-start.12 = (f32[1024,64]{0,1:T(8,128)}, f32[1024,64]{0,1:T(8,128)S(1)}, u32[]{:S(2)}, u32[]{:S(2)}) collective-permute-start(f32[1024,64]{0,1:T(8,128)} %get-tuple-element.13), channel_id=1, source_target_pairs={{0,1},{1,2},{2,3},{3,4},{4,5},{5,6},{6,7},{7,8},{8,9},{9,10},{10,1... | collective-permute-start | bytes 786440 | tf_op jit(solution)/shard_map/ppermute | solution.py:20
  387.0 26.5 %collective-permute-start.13 = (f32[1024,64]{0,1:T(8,128)S(1)}, f32[1024,64]{0,1:T(8,128)S(1)}, u32[]{:S(2)}, u32[]{:S(2)}) collective-permute-start(f32[1024,64]{0,1:T(8,128)S(1)} %get-tuple-element.14), channel_id=1, source_target_pairs={{1,0},{2,1},{3,2},{4,3},{5,4},{6,5},{7,6},{8,7},{9,8},{10,9},{11,1... | collective-permute-start | bytes 786440 | tf_op jit(solution)/shard_map/ppermute | solution.py:23
where the time goes:
time: 577 us; the launch traced here: 575 us
  blocking collectives  382 us (66%)
  matrix products  41.5 us (7%)
  starting transfers between devices  41.4 us (7%)
  local copies, waits for them, and re-layouts  36.2 us (6%)
  waiting for transfers between devices  32.9 us (6%)
  between operations  20.9 us (4%)
  other arithmetic  20.1 us (3%)
    psum x3, blocking collectives, shards(): squares = lax.psum(jnp.sum(vector_new * vector_new), ('site', 'phonon'))  227 us
    psum x1, blocking collectives, shards(): start_squares = lax.psum(jnp.sum(state * state), ('site', 'phonon'))  81.4 us
    psum x1, blocking collectives, shards(): moment = lax.psum(jnp.sum(initial * updated), ('site', 'phonon')) / entries  73.7 us
    dot_general x12, matrix products, shards(): jnp.dot(masked[chosen], flipped.astype(jnp.bfloat16), preferred_element_t...  41.5 us
    ppermute x3, starting transfers between devices, extended_2(): lax.ppermute(lax.slice_in_dim(block, block.shape[dim] - width, None, axis...  17.1 us
    broadcast_in_dim x1, local copies, waits for them, and re-layouts, shards(): jnp.repeat(jnp.repeat(op_mask, block_edge, axis=1), block_edge, axis=2)  14.8 us
    ppermute x12, starting transfers between devices, partner(): return lax.ppermute(value, axis, pairs)  13.4 us
    gt x1, local copies, waits for them, and re-layouts, shards(): masked = jnp.where(expanded > 0, operators, jnp.zeros((), jnp.bfloat16))  12 us
  transfers between devices with their start and end apart: 18, of which 9 were waited for; matrix products, arithmetic and copies ran while one was open for 12% of the time, Pallas kernels for 0%

commit v1 on v0

v1 whole, which is shorter than its diff:
```python
import functools
import jax
import jax.numpy as jnp
from jax import lax
from jax.experimental import pallas as pl
from jax.experimental.pallas import tpu as pltpu
from jax.sharding import PartitionSpec as P

MESH = pl.DeviceIdType.MESH
F32 = jnp.float32
BF16 = jnp.bfloat16
ROWS = 1024
LANES = 128
STEPS = 3
EPSILON = 1e-06
ENTRIES = 33554432.0


def flipped(value, bit):
    size = 8 << bit
    parts = [value[i * size : (i + 1) * size] for i in range(LANES // size)]
    swapped = []
    for i in range(0, len(parts), 2):
        swapped += [parts[i + 1], parts[i]]
    return jnp.concatenate(swapped, axis=0)


def kernel(
    state, ops, mask, site_bits, field, site_coupling, mode_coupling,
    last, prev, moments,
    st, opv, a, t, r_in, r_2, r_3, w_1, w_2, w_3, u_0, u_1, u_2, ub, acc, occ, halo,
    sc_a, sc_b, ss_a, ss_b, out_2, out_3,
    load_sem, self_sem, out_sem, send_sem, recv_sem, hsend_sem, hrecv_sem,
    asend_sem, arecv_sem, bsend_sem, brecv_sem,
):
    site = lax.axis_index("site")
    phonon = lax.axis_index("phonon")
    z_lo, x = site // 4, site % 4
    y, q = phonon // 4, phonon % 4
    z_hi, core = q // 2, q % 2
    z = z_hi * 4 + z_lo
    mode = site * 4 + q
    index_a = x * 8 + y * 2 + core

    load_state = pltpu.make_async_copy(state, st, load_sem.at[0])
    load_state.start()
    load_ops = pltpu.make_async_copy(ops, opv, load_sem.at[1])
    load_ops.start()

    barrier = pltpu.get_barrier_semaphore()

    def plane(k):
        other = (mode + k) % 64
        return other, (other // 4, y * 4 + other % 4)

    def stage_a(k):
        other = (index_a + k) % 32
        return other, (z_lo * 4 + other // 8, ((other // 2) % 4) * 4 + z_hi * 2 + other % 2)

    def stage_b(k):
        other = (z + k) % 8
        return other, ((other % 4) * 4 + x, y * 4 + (other // 4) * 2 + core)

    @pl.loop(1, 64)
    def _(k):
        pl.semaphore_signal(barrier, inc=1, device_id=plane(k)[1], device_id_type=MESH)

    @pl.loop(0, 24)
    def _(k):
        y_other = (y + 1 + k // 8) % 4
        device = (z_lo * 4 + (k // 2) % 4, y_other * 4 + z_hi * 2 + k % 2)
        pl.semaphore_signal(barrier, inc=1, device_id=device, device_id_type=MESH)

    load_state.wait()
    zero = jnp.zeros((8, LANES), F32)
    squares = zero
    for high in range(8):
        block = st[high * 128 : (high + 1) * 128, :]
        squares = squares + jnp.sum((block * block).reshape(16, 8, LANES), axis=0)
        turned = block.T
        t[pl.ds(high, 64, stride=16), :] = turned[:64]
        t[pl.ds(8 + high, 64, stride=16), :] = turned[64:]

    lane = lax.broadcasted_iota(jnp.int32, (1, LANES), 1)

    def fold(value):
        row = jnp.sum(value, axis=0, keepdims=True)
        return row + pltpu.roll(row, 64, 1)

    def spread(src, dst_of, count, target, send, recv, index):
        @pl.loop(1, count)
        def _(k):
            other, device = target(k)
            pltpu.make_async_remote_copy(
                src_ref=src, dst_ref=dst_of(index), send_sem=send, recv_sem=recv,
                device_id=device, device_id_type=MESH,
            ).start()

    def scalars_start(r, squares, products):
        row = jnp.where(lane < 64, fold(squares), fold(products))
        ss_a[r] = row
        sc_a[r, index_a] = row
        spread(ss_a.at[r], lambda i: sc_a.at[r, i], 32, stage_a, asend_sem.at[r], arecv_sem.at[r], index_a)

    def wait_recv(ref, send, recv):
        pltpu.make_async_remote_copy(
            src_ref=ref, dst_ref=ref, send_sem=send, recv_sem=recv,
            device_id=(site, phonon), device_id_type=MESH,
        ).wait_recv()

    def wait_send(ref, send, recv):
        pltpu.make_async_remote_copy(
            src_ref=ref, dst_ref=ref, send_sem=send, recv_sem=recv,
            device_id=(site, phonon), device_id_type=MESH,
        ).wait_send()

    def scalars_middle(r):
        wait_recv(sc_a.at[r, pl.ds(0, 31)], asend_sem.at[r], arecv_sem.at[r])
        row = jnp.sum(sc_a[r], axis=0)
        ss_b[r] = row
        sc_b[r, z] = row
        spread(ss_b.at[r], lambda i: sc_b.at[r, i], 8, stage_b, bsend_sem.at[r], brecv_sem.at[r], z)

    def scalars_end(r):
        wait_recv(sc_b.at[r, pl.ds(0, 7)], bsend_sem.at[r], brecv_sem.at[r])
        row = jnp.sum(sc_b[r], axis=0)
        total = jnp.sum(jnp.where(lane < 64, row, 0.0), axis=1, keepdims=True)
        product = jnp.sum(jnp.where(lane < 64, 0.0, row), axis=1, keepdims=True)
        inverse = 1.0 / jnp.sqrt(total / ENTRIES + EPSILON)
        return inverse, product * inverse / ENTRIES

    def chunk2(ref, i):
        return ref.at[pl.ds(pl.multiple_of(i * 16, 16), 16), :]

    def chunk3(ref, i):
        return ref.at[i // 4, pl.ds(pl.multiple_of((i % 4) * 16, 16), 16), :]

    def exchange_start(e, src, src_chunk, dst, dst_chunk):
        pltpu.make_async_copy(src_chunk(src, mode), dst_chunk(dst, mode), self_sem.at[e]).start()

        @pl.loop(1, 64)
        def _(k):
            other, device = plane(k)
            pltpu.make_async_remote_copy(
                src_ref=src_chunk(src, other), dst_ref=dst_chunk(dst, mode),
                send_sem=send_sem.at[e], recv_sem=recv_sem.at[e],
                device_id=device, device_id_type=MESH,
            ).start()

    def exchange_wait(e, src, src_chunk, dst, dst_chunk):
        pltpu.make_async_copy(src_chunk(src, mode), dst_chunk(dst, mode), self_sem.at[e]).wait()
        wait_recv(t.at[pl.ds(0, 63 * 16), :], send_sem.at[e], recv_sem.at[e])

    def halo_copies(k, w):
        up = pltpu.make_async_remote_copy(
            src_ref=w.at[:, pl.ds(56, 8), :], dst_ref=halo.at[k, 0],
            send_sem=hsend_sem.at[k, 0], recv_sem=hrecv_sem.at[k, 0],
            device_id=(site, ((y + 1) % 4) * 4 + q), device_id_type=MESH,
        )
        down = pltpu.make_async_remote_copy(
            src_ref=w.at[:, pl.ds(0, 8), :], dst_ref=halo.at[k, 1],
            send_sem=hsend_sem.at[k, 1], recv_sem=hrecv_sem.at[k, 1],
            device_id=(site, ((y + 3) % 4) * 4 + q), device_id_type=MESH,
        )
        return up, down

    pl.semaphore_wait(barrier, 87)
    scalars_start(0, squares, zero)
    exchange_start(0, t, chunk2, r_in, chunk3)

    chosen = [site_bits[b] for b in range(4)]
    fields = [field[c] for c in chosen]
    device_coupling = [site_coupling[c] for c in chosen]

    place = lax.broadcasted_iota(jnp.int32, (8, ROWS), 1)
    weights = jnp.zeros((8, ROWS), F32)
    for j in range(10):
        weights = weights + site_coupling[4 + j] * ((place >> j) & 1).astype(F32)
    occ[...] = weights

    level = lax.broadcasted_iota(jnp.int32, (8, LANES), 0) + y * 8
    mode_weight = mode_coupling[mode] / jnp.sqrt(F32(32.0))
    lower_weight = mode_weight * jnp.sqrt(level.astype(F32))
    upper_weight = mode_weight * jnp.where(level < 31, jnp.sqrt((level + 1).astype(F32)), 0.0)

    load_ops.wait()

    def mask_operator(b):
        @pl.loop(0, 8)
        def _(i):
            rows = pl.ds(pl.multiple_of(i * 128, 128), 128)
            for j in range(8):
                keep = mask[chosen[b] * 64 + i * 8 + j] > 0
                tile = opv[chosen[b], rows, j * 128 : (j + 1) * 128]
                a[b, rows, j * 128 : (j + 1) * 128] = jnp.where(keep, tile, jnp.zeros_like(tile))

    for b in range(4):
        mask_operator(b)
    scalars_middle(0)
    exchange_wait(0, t, chunk2, r_in, chunk3)
    for copy in halo_copies(0, r_in):
        copy.start()
    inverse, _ = scalars_end(0)

    sublane = lax.broadcasted_iota(jnp.int32, (8, LANES), 0)

    def normalize(w, u, inverse):
        scale = jnp.broadcast_to(inverse, (8, LANES))

        @pl.loop(0, 8)
        def _(e):
            for high in range(8):
                cols = slice(high * 128, (high + 1) * 128)
                first = w[2 * e, pl.ds(high, 8, stride=8), :] * scale
                second = w[2 * e + 1, pl.ds(high, 8, stride=8), :] * scale
                both = jnp.concatenate([first, second], axis=0)
                rows = pl.ds(pl.multiple_of(e * 16, 16), 16)
                u[rows, cols] = both
                ub[rows, cols] = both.astype(BF16)

    def step(k, u, u_before, w, inverse):
        scale = jnp.broadcast_to(inverse, (8, LANES))

        @pl.loop(0, 4)
        def _(c):
            cols = pl.ds(pl.multiple_of(c * 256, 256), 256)
            here = u[:, cols]
            total = None
            for b in range(4):
                product = lax.dot_general(
                    ub[...], a[b, cols, :], (((1,), (1,)), ((), ())), preferred_element_type=F32
                )
                moved = flipped(product + fields[b] * here, b)
                total = moved if total is None else total + moved
            acc[:, cols] = total

        for copy in halo_copies(k, w):
            copy.wait_recv()

        def body(d, carry):
            squares, products = carry
            constant = F32(0.0)
            for b in range(4):
                constant = constant + device_coupling[b] * ((d >> b) & 1).astype(F32)
            rows = pl.ds(pl.multiple_of(d * 8, 8), 8)
            for high in range(8):
                cols = slice(high * 128, (high + 1) * 128)
                here = u[rows, cols]
                below = jnp.broadcast_to(halo[k, 0, d, high : high + 1, :], (8, LANES)) * scale
                above = jnp.broadcast_to(halo[k, 1, d, high : high + 1, :], (8, LANES)) * scale
                lower = jnp.where(sublane == 0, below, pltpu.roll(here, 1, 0))
                upper = jnp.where(sublane == 7, above, pltpu.roll(here, 7, 0))
                ladder = (occ[:, cols] + constant) * (lower_weight * lower + upper_weight * upper)
                new = acc[rows, cols] + ladder
                if k > 0:
                    new = 2.0 * new - u_before[rows, cols] * scale
                w[d, pl.ds(high, 8, stride=8), :] = new
                squares = squares + new * new
                products = products + u_0[rows, cols] * new
            return squares, products

        return lax.fori_loop(0, 16, body, (zero, zero))

    def finish(r, inverse, out):
        scale = jnp.broadcast_to(inverse, (128, LANES))
        for high in range(8):
            block = jnp.concatenate(
                [r[pl.ds(high, 64, stride=16), :], r[pl.ds(8 + high, 64, stride=16), :]], axis=0
            )
            out[high * 128 : (high + 1) * 128, :] = block.T * scale

    def set_moment(k, value):
        moments[k] = value[0, 0]

    normalize(r_in, u_0, inverse)
    squares, products = step(0, u_0, u_0, w_1, inverse)
    scalars_start(1, squares, products)
    for copy in halo_copies(1, w_1):
        copy.start()
    scalars_middle(1)
    inverse, moment = scalars_end(1)
    set_moment(0, moment)

    normalize(w_1, u_1, inverse)
    squares, products = step(1, u_1, u_0, w_2, inverse)
    scalars_start(2, squares, products)
    for copy in halo_copies(2, w_2):
        copy.start()
    scalars_middle(2)
    inverse, moment = scalars_end(2)
    exchange_start(1, w_2, chunk3, r_2, chunk2)
    set_moment(1, moment)
    inverse_2 = inverse

    normalize(w_2, u_2, inverse)
    squares, products = step(2, u_2, u_1, w_3, inverse)
    scalars_start(3, squares, products)
    exchange_start(2, w_3, chunk3, r_3, chunk2)
    scalars_middle(3)
    exchange_wait(1, w_2, chunk3, r_2, chunk2)
    finish(r_2, inverse_2, out_2)
    store_2 = pltpu.make_async_copy(out_2, prev, out_sem.at[0])
    store_2.start()
    inverse, moment = scalars_end(3)
    set_moment(2, moment)
    exchange_wait(2, w_3, chunk3, r_3, chunk2)
    finish(r_3, inverse, out_3)
    store_3 = pltpu.make_async_copy(out_3, last, out_sem.at[1])
    store_3.start()

    for e in range(3):
        wait_send(t.at[pl.ds(0, 63 * 16), :], send_sem.at[e], recv_sem.at[e])
    for r in range(4):
        wait_send(sc_a.at[r, pl.ds(0, 31)], asend_sem.at[r], arecv_sem.at[r])
        wait_send(sc_b.at[r, pl.ds(0, 7)], bsend_sem.at[r], brecv_sem.at[r])
    for k, w in enumerate((r_in, w_1, w_2)):
        for copy in halo_copies(k, w):
            copy.wait_send()
    store_2.wait()
    store_3.wait()


def shards(state, operators, op_mask, site_bits, field, site_coupling, mode_coupling):
    block = jax.ShapeDtypeStruct((ROWS, LANES), F32)
    flat = pltpu.VMEM((ROWS, LANES), F32)
    cube = pltpu.VMEM((16, 64, LANES), F32)
    wide = pltpu.VMEM((LANES, ROWS), F32)
    dma = pltpu.SemaphoreType.DMA
    anywhere = pl.BlockSpec(memory_space=pl.ANY)
    scalar = pl.BlockSpec(memory_space=pltpu.SMEM)
    return pl.pallas_call(
        kernel,
        out_shape=(block, block, jax.ShapeDtypeStruct((STEPS,), F32)),
        in_specs=[anywhere, anywhere, scalar, scalar, scalar, scalar, scalar],
        out_specs=(anywhere, anywhere, scalar),
        scratch_shapes=[
            flat,
            pltpu.VMEM((4, ROWS, ROWS), BF16),
            pltpu.VMEM((4, ROWS, ROWS), BF16),
            flat,
            cube,
            flat,
            flat,
            cube,
            cube,
            cube,
            wide,
            wide,
            wide,
            pltpu.VMEM((LANES, ROWS), BF16),
            wide,
            pltpu.VMEM((8, ROWS), F32),
            pltpu.VMEM((3, 2, 16, 8, LANES), F32),
            pltpu.VMEM((4, 32, 1, LANES), F32),
            pltpu.VMEM((4, 8, 1, LANES), F32),
            pltpu.VMEM((4, 1, LANES), F32),
            pltpu.VMEM((4, 1, LANES), F32),
            flat,
            flat,
            dma((2,)),
            dma((3,)),
            dma((2,)),
            dma((3,)),
            dma((3,)),
            dma((3, 2)),
            dma((3, 2)),
            dma((4,)),
            dma((4,)),
            dma((4,)),
            dma((4,)),
        ],
        compiler_params=pltpu.CompilerParams(
            collective_id=0, has_side_effects=True, vmem_limit_bytes=48 * 1024 * 1024
        ),
    )(state, operators, op_mask.reshape(-1), site_bits, field, site_coupling, mode_coupling)


def solution(mesh):
    in_specs = (P("site", "phonon"), P(), P(), P(), P(), P(), P())
    out_specs = (P("site", "phonon"), P("site", "phonon"), P())
    return jax.shard_map(shards, mesh=mesh, in_specs=in_specs, out_specs=out_specs, check_vma=False)
```

time: 577 us -> 91.8 us (0.16)
  blocking collectives: 382 us -> 0 us
  Pallas kernels: 0 us -> 84.4 us
  matrix products: 41.5 us -> 0 us
  starting transfers between devices: 41.4 us -> 0 us
  waiting for transfers between devices: 32.9 us -> 0 us
  local copies, waits for them, and re-layouts: 36.2 us -> 6.56 us
  between operations: 20.9 us -> 0.65 us
  other arithmetic: 20.1 us -> 0 us
    psum x5 -> x0, blocking collectives: 382 us -> none  [the longest x3 227 us: shards(): squares = lax.psum(jnp.sum(vector_new * vector_new), ('site', 'phonon'))]
    pallas_call x0 -> x1, Pallas kernels: none -> 84.4 us  [shards(): pl.pallas_call(kernel, out_shape=(block, block, jax.ShapeDtypeStruct((STE...]
    dot_general x12 -> x0, matrix products: 41.5 us -> none  [shards(): jnp.dot(masked[chosen], flipped.astype(jnp.bfloat16), preferred_element_t...]
    ppermute x18 -> x0, starting transfers between devices: 41.4 us -> none  [the longest x3 17.1 us: extended_2(): lax.ppermute(lax.slice_in_dim(block, block.shape[dim] - width, None, axis...]
    ppermute x18 -> x0, waiting for transfers between devices: 32.9 us -> none  [the longest x12 12 us: partner(): return lax.ppermute(value, axis, pairs)]
    broadcast_in_dim x2 -> x0, local copies, waits for them, and re-layouts: 14.9 us -> none  [the longest x1 14.8 us: shards(): jnp.repeat(jnp.repeat(op_mask, block_edge, axis=1), block_edge, axis=2)]
    gt x1 -> x0, local copies, waits for them, and re-layouts: 12 us -> none  [shards(): masked = jnp.where(expanded > 0, operators, jnp.zeros((), jnp.bfloat16))]
    select_n x1 -> x0, other arithmetic: 8.7 us -> none  [shards(): masked = jnp.where(expanded > 0, operators, jnp.zeros((), jnp.bfloat16))]
  transfers between devices with their start and end apart: 18 -> 0, of which waited for: 9 -> 0; matrix products, arithmetic and copies ran while one was open for 12% -> 0% of each run, Pallas kernels for 0% -> 0%
where the time goes in v1:
time: 91.8 us; the launch traced here: 91.6 us
  Pallas kernels  84.4 us (92%)
  local copies, waits for them, and re-layouts  6.56 us (7%)
    pallas_call x1, Pallas kernels, shards(): pl.pallas_call(kernel, out_shape=(block, block, jax.ShapeDtypeStruct((STE...  84.4 us
    unnamed x13, local copies, waits for them, and re-layouts  5.76 us

profile of v1, /device:TPU:1, one launch (start us, length us, event | category | flops | bytes accessed | tf_op | source)
XLA Modules:
  0.0 91.6 jit_solution(14898802532683581255)
XLA Ops:
  0.6 0.8 reshape.9.mask
  1.4 0.0 copy-start
  1.4 1.0 %copy-done = f32[1024,128]{1,0:T(8,128)S(1)} copy-done((f32[1024,128]{1,0:T(8,128)S(1)}, f32[1024,128]{1,0:T(8,128)}, u32[]{:S(2)}) %copy-start) | copy-done | bytes 524312
  2.5 0.0 copy-start.1
  2.5 0.7 copy-done.1
  3.1 0.0 copy-start.2
  3.1 0.7 copy-done.2
  3.8 0.0 copy-start.3
  3.8 0.7 copy-done.3
  4.4 0.0 copy-start.4
  4.5 0.7 copy-done.4
  5.1 84.4 %shard_map.94 = (f32[1024,128]{1,0:T(8,128)S(1)}, f32[1024,128]{1,0:T(8,128)S(1)}, f32[3]{0:T(128)S(1)}) custom-call(f32[1024,128]{1,0:T(8,128)S(1)} %copy-done, bf16[4,1024,1024]{2,1,0:T(8,128)(2,1)} %ops.1, s32[256]{0:T(256)S(1)} %reshape.9.mask, s32[4]{0:T(128)S(1)} %copy-done.1, f32[4]{0:T(128)S(1)} %copy-done.2, f32[14]{0:T(128)S(1)} %copy-done.3, ...), custom_call_target="tpu_custom_call" | custom-call | tf_op jit(solution)/shard_map/pallas_call | solution.py:331
  89.5 0.8 copy.13
  90.3 0.8 copy.14
  91.1 0.5 copy.15
Async XLA Ops:
  1.4 1.0 %copy-start = (f32[1024,128]{1,0:T(8,128)S(1)}, f32[1024,128]{1,0:T(8,128)}, u32[]{:S(2)}) copy-start(f32[1024,128]{1,0:T(8,128)} %state.1) | copy-start | bytes 1572868
  2.5 0.7 copy-start.1
  3.1 0.7 copy-start.2
  3.8 0.7 copy-start.3
  4.4 0.7 copy-start.4

commit v2 on v1

--- a/solution.py
+++ b/solution.py
@@ -25,13 +25,36 @@
     return jnp.concatenate(swapped, axis=0)
 
 
+def ring(offset, size):
+    return min(offset % size, -offset % size)
+
+
+def offsets(zs=1, xs=1, ys=1, cores=1):
+    found = [
+        (dz, dx, dy, dc)
+        for dz in range(zs)
+        for dx in range(xs)
+        for dy in range(ys)
+        for dc in range(cores)
+        if (dz, dx, dy, dc) != (0, 0, 0, 0)
+    ]
+    return sorted(found, key=lambda o: -ring(o[0], 8) - ring(o[1], 4) - ring(o[2], 4))
+
+
+PLANE = offsets(zs=8, xs=4, cores=2)
+LINE = offsets(ys=4)
+COLUMN = offsets(zs=8, cores=2)
+LAYER = offsets(xs=4, ys=4)
+
+
 def kernel(
-    state, ops, mask, site_bits, field, site_coupling, mode_coupling,
+    state, ops, mask_in, site_bits_in, field_in, site_coupling_in, mode_coupling_in,
     last, prev, moments,
+    mask, site_bits, field, site_coupling, mode_coupling,
     st, opv, a, t, r_in, r_2, r_3, w_1, w_2, w_3, u_0, u_1, u_2, ub, acc, occ, halo,
-    sc_a, sc_b, ss_a, ss_b, out_2, out_3,
+    slots_1, slots_2, rows_1, rows_2, out_2, out_3,
     load_sem, self_sem, out_sem, send_sem, recv_sem, hsend_sem, hrecv_sem,
-    asend_sem, arecv_sem, bsend_sem, brecv_sem,
+    send_1, recv_1, send_2, recv_2,
 ):
     site = lax.axis_index("site")
     phonon = lax.axis_index("phonon")
@@ -40,36 +63,38 @@
     z_hi, core = q // 2, q % 2
     z = z_hi * 4 + z_lo
     mode = site * 4 + q
-    index_a = x * 8 + y * 2 + core
+
+    def place_of(offset):
+        dz, dx, dy, dc = offset
+        z_at, x_at, y_at, core_at = (z + dz) % 8, (x + dx) % 4, (y + dy) % 4, (core + dc) % 2
+        return (z_at % 4) * 4 + x_at, y_at, (z_at // 4) * 2 + core_at
+
+    def device_of(offset):
+        site_at, y_at, q_at = place_of(offset)
+        return (site_at, y_at * 4 + q_at)
+
+    barrier = pltpu.get_barrier_semaphore()
+    for offset in PLANE + LINE:
+        pl.semaphore_signal(barrier, inc=1, device_id=device_of(offset), device_id_type=MESH)
 
     load_state = pltpu.make_async_copy(state, st, load_sem.at[0])
     load_state.start()
     load_ops = pltpu.make_async_copy(ops, opv, load_sem.at[1])
+    small = [
+        pltpu.make_async_copy(source, target, load_sem.at[2 + i])
+        for i, (source, target) in enumerate(
+            (
+                (mask_in, mask),
+                (site_bits_in, site_bits),
+                (field_in, field),
+                (site_coupling_in, site_coupling),
+                (mode_coupling_in, mode_coupling),
+            )
+        )
+    ]
+    for copy in small:
+        copy.start()
     load_ops.start()
-
-    barrier = pltpu.get_barrier_semaphore()
-
-    def plane(k):
-        other = (mode + k) % 64
-        return other, (other // 4, y * 4 + other % 4)
-
-    def stage_a(k):
-        other = (index_a + k) % 32
-        return other, (z_lo * 4 + other // 8, ((other // 2) % 4) * 4 + z_hi * 2 + other % 2)
-
-    def stage_b(k):
-        other = (z + k) % 8
-        return other, ((other % 4) * 4 + x, y * 4 + (other // 4) * 2 + core)
-
-    @pl.loop(1, 64)
-    def _(k):
-        pl.semaphore_signal(barrier, inc=1, device_id=plane(k)[1], device_id_type=MESH)
-
-    @pl.loop(0, 24)
-    def _(k):
-        y_other = (y + 1 + k // 8) % 4
-        device = (z_lo * 4 + (k // 2) % 4, y_other * 4 + z_hi * 2 + k % 2)
-        pl.semaphore_signal(barrier, inc=1, device_id=device, device_id_type=MESH)
 
     load_state.wait()
     zero = jnp.zeros((8, LANES), F32)
@@ -87,21 +112,6 @@
         row = jnp.sum(value, axis=0, keepdims=True)
         return row + pltpu.roll(row, 64, 1)
 
-    def spread(src, dst_of, count, target, send, recv, index):
-        @pl.loop(1, count)
-        def _(k):
-            other, device = target(k)
-            pltpu.make_async_remote_copy(
-                src_ref=src, dst_ref=dst_of(index), send_sem=send, recv_sem=recv,
-                device_id=device, device_id_type=MESH,
-            ).start()
-
-    def scalars_start(r, squares, products):
-        row = jnp.where(lane < 64, fold(squares), fold(products))
-        ss_a[r] = row
-        sc_a[r, index_a] = row
-        spread(ss_a.at[r], lambda i: sc_a.at[r, i], 32, stage_a, asend_sem.at[r], arecv_sem.at[r], index_a)
-
     def wait_recv(ref, send, recv):
         pltpu.make_async_remote_copy(
             src_ref=ref, dst_ref=ref, send_sem=send, recv_sem=recv,
@@ -114,16 +124,38 @@
             device_id=(site, phonon), device_id_type=MESH,
         ).wait_send()
 
-    def scalars_middle(r):
-        wait_recv(sc_a.at[r, pl.ds(0, 31)], asend_sem.at[r], arecv_sem.at[r])
-        row = jnp.sum(sc_a[r], axis=0)
-        ss_b[r] = row
-        sc_b[r, z] = row
-        spread(ss_b.at[r], lambda i: sc_b.at[r, i], 8, stage_b, bsend_sem.at[r], brecv_sem.at[r], z)
-
-    def scalars_end(r):
-        wait_recv(sc_b.at[r, pl.ds(0, 7)], bsend_sem.at[r], brecv_sem.at[r])
-        row = jnp.sum(sc_b[r], axis=0)
+    groups = {
+        "plane": (PLANE, 64, site * 4 + q),
+        "line": (LINE, 4, y),
+        "column": (COLUMN, 16, z * 2 + core),
+        "layer": (LAYER, 16, x * 4 + y),
+    }
+
+    def spread(group, src, slots, row, send, recv):
+        members, count, index = groups[group]
+        src[...] = row
+        slots[index] = row
+        for offset in members:
+            pltpu.make_async_remote_copy(
+                src_ref=src, dst_ref=slots.at[index], send_sem=send, recv_sem=recv,
+                device_id=device_of(offset), device_id_type=MESH,
+            ).start()
+
+    def gather(group, slots, send, recv):
+        members, count, index = groups[group]
+        wait_recv(slots.at[pl.ds(0, count - 1)], send, recv)
+        return jnp.sum(slots[0:count], axis=0)
+
+    def scalars_start(r, group, squares, products):
+        row = jnp.where(lane < 64, fold(squares), fold(products))
+        spread(group, rows_1.at[r], slots_1.at[r], row, send_1.at[r], recv_1.at[r])
+
+    def scalars_middle(r, group, group_2):
+        row = gather(group, slots_1.at[r], send_1.at[r], recv_1.at[r])
+        spread(group_2, rows_2.at[r], slots_2.at[r], row, send_2.at[r], recv_2.at[r])
+
+    def scalars_end(r, group_2):
+        row = gather(group_2, slots_2.at[r], send_2.at[r], recv_2.at[r])
         total = jnp.sum(jnp.where(lane < 64, row, 0.0), axis=1, keepdims=True)
         product = jnp.sum(jnp.where(lane < 64, 0.0, row), axis=1, keepdims=True)
         inverse = 1.0 / jnp.sqrt(total / ENTRIES + EPSILON)
@@ -132,23 +164,41 @@
     def chunk2(ref, i):
         return ref.at[pl.ds(pl.multiple_of(i * 16, 16), 16), :]
 
-    def chunk3(ref, i):
-        return ref.at[i // 4, pl.ds(pl.multiple_of((i % 4) * 16, 16), 16), :]
-
-    def exchange_start(e, src, src_chunk, dst, dst_chunk):
-        pltpu.make_async_copy(src_chunk(src, mode), dst_chunk(dst, mode), self_sem.at[e]).start()
-
-        @pl.loop(1, 64)
-        def _(k):
-            other, device = plane(k)
+    def chunk3(ref, site_at, q_at):
+        return ref.at[site_at, pl.ds(pl.multiple_of(q_at * 16, 16), 16), :]
+
+    def exchange_in_self():
+        return pltpu.make_async_copy(chunk2(t, mode), chunk3(r_in, site, q), self_sem.at[0])
+
+    def exchange_in_start():
+        exchange_in_self().start()
+        for offset in PLANE:
+            site_at, y_at, q_at = place_of(offset)
             pltpu.make_async_remote_copy(
-                src_ref=src_chunk(src, other), dst_ref=dst_chunk(dst, mode),
+                src_ref=chunk2(t, site_at * 4 + q_at), dst_ref=chunk3(r_in, site, q),
+                send_sem=send_sem.at[0], recv_sem=recv_sem.at[0],
+                device_id=(site_at, y_at * 4 + q_at), device_id_type=MESH,
+            ).start()
+
+    def exchange_in_wait():
+        exchange_in_self().wait()
+        wait_recv(t.at[pl.ds(0, 63 * 16), :], send_sem.at[0], recv_sem.at[0])
+
+    def exchange_out_self(e, w, r):
+        return pltpu.make_async_copy(chunk3(w, site, q), chunk2(r, mode), self_sem.at[e])
+
+    def exchange_out_start(e, w, r):
+        exchange_out_self(e, w, r).start()
+        for offset in PLANE:
+            site_at, y_at, q_at = place_of(offset)
+            pltpu.make_async_remote_copy(
+                src_ref=chunk3(w, site_at, q_at), dst_ref=chunk2(r, mode),
                 send_sem=send_sem.at[e], recv_sem=recv_sem.at[e],
-                device_id=device, device_id_type=MESH,
+                device_id=(site_at, y_at * 4 + q_at), device_id_type=MESH,
             ).start()
 
-    def exchange_wait(e, src, src_chunk, dst, dst_chunk):
-        pltpu.make_async_copy(src_chunk(src, mode), dst_chunk(dst, mode), self_sem.at[e]).wait()
+    def exchange_out_wait(e, w, r):
+        exchange_out_self(e, w, r).wait()
         wait_recv(t.at[pl.ds(0, 63 * 16), :], send_sem.at[e], recv_sem.at[e])
 
     def halo_copies(k, w):
@@ -164,10 +214,12 @@
         )
         return up, down
 
-    pl.semaphore_wait(barrier, 87)
-    scalars_start(0, squares, zero)
-    exchange_start(0, t, chunk2, r_in, chunk3)
-
+    pl.semaphore_wait(barrier, 66)
+    scalars_start(0, "plane", squares, zero)
+    exchange_in_start()
+
+    for copy in small:
+        copy.wait()
     chosen = [site_bits[b] for b in range(4)]
     fields = [field[c] for c in chosen]
     device_coupling = [site_coupling[c] for c in chosen]
@@ -190,17 +242,17 @@
         def _(i):
             rows = pl.ds(pl.multiple_of(i * 128, 128), 128)
             for j in range(8):
-                keep = mask[chosen[b] * 64 + i * 8 + j] > 0
+                keep = mask[chosen[b], i, j] > 0
                 tile = opv[chosen[b], rows, j * 128 : (j + 1) * 128]
                 a[b, rows, j * 128 : (j + 1) * 128] = jnp.where(keep, tile, jnp.zeros_like(tile))
 
     for b in range(4):
         mask_operator(b)
-    scalars_middle(0)
-    exchange_wait(0, t, chunk2, r_in, chunk3)
+    scalars_middle(0, "plane", "line")
+    exchange_in_wait()
     for copy in halo_copies(0, r_in):
         copy.start()
-    inverse, _ = scalars_end(0)
+    inverse, _ = scalars_end(0, "line")
 
     sublane = lax.broadcasted_iota(jnp.int32, (8, LANES), 0)
 
@@ -218,7 +270,7 @@
                 u[rows, cols] = both
                 ub[rows, cols] = both.astype(BF16)
 
-    def step(k, u, u_before, w, inverse):
+    def step(k, u, u_before, w, inverse, send=None):
         scale = jnp.broadcast_to(inverse, (8, LANES))
 
         @pl.loop(0, 4)
@@ -237,8 +289,9 @@
         for copy in halo_copies(k, w):
             copy.wait_recv()
 
-        def body(d, carry):
+        def body(i, carry):
             squares, products = carry
+            d = (site + 1 + i) % 16
             constant = F32(0.0)
             for b in range(4):
                 constant = constant + device_coupling[b] * ((d >> b) & 1).astype(F32)
@@ -257,6 +310,8 @@
                 w[d, pl.ds(high, 8, stride=8), :] = new
                 squares = squares + new * new
                 products = products + u_0[rows, cols] * new
+            if send is not None:
+                send(i)
             return squares, products
 
         return lax.fori_loop(0, 16, body, (zero, zero))
@@ -274,45 +329,66 @@
 
     normalize(r_in, u_0, inverse)
     squares, products = step(0, u_0, u_0, w_1, inverse)
-    scalars_start(1, squares, products)
+    scalars_start(1, "column", squares, products)
     for copy in halo_copies(1, w_1):
         copy.start()
-    scalars_middle(1)
-    inverse, moment = scalars_end(1)
+    scalars_middle(1, "column", "layer")
+    inverse, moment = scalars_end(1, "layer")
     set_moment(0, moment)
 
     normalize(w_1, u_1, inverse)
     squares, products = step(1, u_1, u_0, w_2, inverse)
-    scalars_start(2, squares, products)
+    scalars_start(2, "column", squares, products)
     for copy in halo_copies(2, w_2):
         copy.start()
-    scalars_middle(2)
-    inverse, moment = scalars_end(2)
-    exchange_start(1, w_2, chunk3, r_2, chunk2)
+    exchange_out_start(1, w_2, r_2)
+    scalars_middle(2, "column", "layer")
+    inverse, moment = scalars_end(2, "layer")
     set_moment(1, moment)
     inverse_2 = inverse
 
+    def send_ready(i):
+        @pl.when(i > 0)
+        def _():
+            d = (site + i) % 16
+            for q_at in range(4):
+                pltpu.make_async_remote_copy(
+                    src_ref=chunk3(w_3, d, q_at), dst_ref=chunk2(r_3, mode),
+                    send_sem=send_sem.at[2], recv_sem=recv_sem.at[2],
+                    device_id=(d, y * 4 + q_at), device_id_type=MESH,
+                ).start()
+
     normalize(w_2, u_2, inverse)
-    squares, products = step(2, u_2, u_1, w_3, inverse)
-    scalars_start(3, squares, products)
-    exchange_start(2, w_3, chunk3, r_3, chunk2)
-    scalars_middle(3)
-    exchange_wait(1, w_2, chunk3, r_2, chunk2)
+    squares, products = step(2, u_2, u_1, w_3, inverse, send_ready)
+    for j in range(1, 4):
+        q_at = (q + j) % 4
+        pltpu.make_async_remote_copy(
+            src_ref=chunk3(w_3, site, q_at), dst_ref=chunk2(r_3, mode),
+            send_sem=send_sem.at[2], recv_sem=recv_sem.at[2],
+            device_id=(site, y * 4 + q_at), device_id_type=MESH,
+        ).start()
+    exchange_out_self(2, w_3, r_3).start()
+    scalars_start(3, "layer", squares, products)
+    scalars_middle(3, "layer", "column")
+    exchange_out_wait(1, w_2, r_2)
     finish(r_2, inverse_2, out_2)
     store_2 = pltpu.make_async_copy(out_2, prev, out_sem.at[0])
     store_2.start()
-    inverse, moment = scalars_end(3)
+    inverse, moment = scalars_end(3, "column")
     set_moment(2, moment)
-    exchange_wait(2, w_3, chunk3, r_3, chunk2)
+    exchange_out_wait(2, w_3, r_3)
     finish(r_3, inverse, out_3)
     store_3 = pltpu.make_async_copy(out_3, last, out_sem.at[1])
     store_3.start()
 
     for e in range(3):
         wait_send(t.at[pl.ds(0, 63 * 16), :], send_sem.at[e], recv_sem.at[e])
-    for r in range(4):
-        wait_send(sc_a.at[r, pl.ds(0, 31)], asend_sem.at[r], arecv_sem.at[r])
-        wait_send(sc_b.at[r, pl.ds(0, 7)], bsend_sem.at[r], brecv_sem.at[r])
+    for r, (group, group_2) in enumerate(
+        (("plane", "line"), ("column", "layer"), ("column", "layer"), ("layer", "column"))
+    ):
+        count, count_2 = groups[group][1], groups[group_2][1]
+        wait_send(slots_1.at[r, pl.ds(0, count - 1)], send_1.at[r], recv_1.at[r])
+        wait_send(slots_2.at[r, pl.ds(0, count_2 - 1)], send_2.at[r], recv_2.at[r])
     for k, w in enumerate((r_in, w_1, w_2)):
         for copy in halo_copies(k, w):
             copy.wait_send()
@@ -327,13 +403,19 @@
     wide = pltpu.VMEM((LANES, ROWS), F32)
     dma = pltpu.SemaphoreType.DMA
     anywhere = pl.BlockSpec(memory_space=pl.ANY)
+    hbm = pl.BlockSpec(memory_space=pltpu.HBM)
     scalar = pl.BlockSpec(memory_space=pltpu.SMEM)
     return pl.pallas_call(
         kernel,
         out_shape=(block, block, jax.ShapeDtypeStruct((STEPS,), F32)),
-        in_specs=[anywhere, anywhere, scalar, scalar, scalar, scalar, scalar],
+        in_specs=[hbm] * 7,
         out_specs=(anywhere, anywhere, scalar),
         scratch_shapes=[
+            pltpu.SMEM((4, 8, 8), jnp.int32),
+            pltpu.SMEM((4,), jnp.int32),
+            pltpu.SMEM((4,), F32),
+            pltpu.SMEM((14,), F32),
+            pltpu.SMEM((64,), F32),
             flat,
             pltpu.VMEM((4, ROWS, ROWS), BF16),
             pltpu.VMEM((4, ROWS, ROWS), BF16),
@@ -351,13 +433,13 @@
             wide,
             pltpu.VMEM((8, ROWS), F32),
             pltpu.VMEM((3, 2, 16, 8, LANES), F32),
-            pltpu.VMEM((4, 32, 1, LANES), F32),
-            pltpu.VMEM((4, 8, 1, LANES), F32),
+            pltpu.VMEM((4, 64, 1, LANES), F32),
+            pltpu.VMEM((4, 16, 1, LANES), F32),
             pltpu.VMEM((4, 1, LANES), F32),
             pltpu.VMEM((4, 1, LANES), F32),
             flat,
             flat,
-            dma((2,)),
+            dma((7,)),
             dma((3,)),
             dma((2,)),
             dma((3,)),
@@ -372,7 +454,7 @@
         compiler_params=pltpu.CompilerParams(
             collective_id=0, has_side_effects=True, vmem_limit_bytes=48 * 1024 * 1024
         ),
-    )(state, operators, op_mask.reshape(-1), site_bits, field, site_coupling, mode_coupling)
+    )(state, operators, op_mask, site_bits, field, site_coupling, mode_coupling)
 
 
 def solution(mesh):

time: 91.8 us -> 81.1 us (0.88)
  Pallas kernels: 84.4 us -> 73.8 us
    pallas_call x1, Pallas kernels: 84.4 us -> 73.8 us  [shards(): pl.pallas_call(kernel, out_shape=(block, block, jax.ShapeDtypeStruct((STE...]
    unnamed x13 -> x15, local copies, waits for them, and re-layouts: 5.76 us -> 6.47 us
where the time goes in v2:
time: 81.1 us; the launch traced here: 80.9 us
  Pallas kernels  73.8 us (91%)
  local copies, waits for them, and re-layouts  6.47 us (8%)
    pallas_call x1, Pallas kernels, shards(): pl.pallas_call(kernel, out_shape=(block, block, jax.ShapeDtypeStruct((STE...  73.8 us
    unnamed x15, local copies, waits for them, and re-layouts  6.47 us

profile of v2, /device:TPU:1, one launch (start us, length us, event | category | flops | bytes accessed | tf_op | source)
XLA Modules:
  0.0 80.9 jit_solution(208601431518409947)
XLA Ops:
  0.6 0.0 copy-start
  0.6 1.0 %copy-done = f32[1024,128]{1,0:T(8,128)S(1)} copy-done((f32[1024,128]{1,0:T(8,128)S(1)}, f32[1024,128]{1,0:T(8,128)}, u32[]{:S(2)}) %copy-start) | copy-done | bytes 524312
  1.7 0.0 copy-start.1
  1.7 0.7 copy-done.1
  2.4 0.0 copy-start.2
  2.4 0.7 copy-done.2
  3.0 0.0 copy-start.3
  3.1 0.7 copy-done.3
  3.7 0.0 copy-start.4
  3.7 0.7 copy-done.4
  4.4 0.0 copy-start.5
  4.4 0.7 copy-done.5
  5.0 73.8 %shard_map.94 = (f32[1024,128]{1,0:T(8,128)S(1)}, f32[1024,128]{1,0:T(8,128)S(1)}, f32[3]{0:T(128)S(1)}) custom-call(f32[1024,128]{1,0:T(8,128)S(1)} %copy-done, bf16[4,1024,1024]{2,1,0:T(8,128)(2,1)} %ops.1, s32[4,8,8]{2,1,0:T(8,128)S(1)} %copy-done.1, s32[4]{0:T(128)S(1)} %copy-done.2, f32[4]{0:T(128)S(1)} %copy-done.3, f32[14]{0:T(128)S(1)} %copy-done.4, ...), custom_call_target="tpu_custom_call" | custom-call | tf_op jit(solution)/shard_map/pallas_call | solution.py:408
  78.8 0.8 copy.13
  79.6 0.8 copy.14
  80.4 0.5 copy.15
Async XLA Ops:
  0.6 1.0 %copy-start = (f32[1024,128]{1,0:T(8,128)S(1)}, f32[1024,128]{1,0:T(8,128)}, u32[]{:S(2)}) copy-start(f32[1024,128]{1,0:T(8,128)} %state.1) | copy-start | bytes 1572868
  1.7 0.7 copy-start.1
  2.4 0.7 copy-start.2
  3.0 0.7 copy-start.3
  3.7 0.7 copy-start.4
  4.4 0.7 copy-start.5

commit v3 on v2

--- a/solution.py
+++ b/solution.py
@@ -45,6 +45,7 @@
 LINE = offsets(ys=4)
 COLUMN = offsets(zs=8, cores=2)
 LAYER = offsets(xs=4, ys=4)
+WHOLE = offsets(zs=8, xs=4, ys=4, cores=2)
 
 
 def kernel(
@@ -52,7 +53,7 @@
     last, prev, moments,
     mask, site_bits, field, site_coupling, mode_coupling,
     st, opv, a, t, r_in, r_2, r_3, w_1, w_2, w_3, u_0, u_1, u_2, ub, acc, occ, halo,
-    slots_1, slots_2, rows_1, rows_2, out_2, out_3,
+    slots_1, slots_2, slots_whole, rows_1, rows_2, out_2, out_3,
     load_sem, self_sem, out_sem, send_sem, recv_sem, hsend_sem, hrecv_sem,
     send_1, recv_1, send_2, recv_2,
 ):
@@ -129,6 +130,7 @@
         "line": (LINE, 4, y),
         "column": (COLUMN, 16, z * 2 + core),
         "layer": (LAYER, 16, x * 4 + y),
+        "whole": (WHOLE, 256, site * 16 + phonon),
     }
 
     def spread(group, src, slots, row, send, recv):
@@ -155,7 +157,9 @@
         spread(group_2, rows_2.at[r], slots_2.at[r], row, send_2.at[r], recv_2.at[r])
 
     def scalars_end(r, group_2):
-        row = gather(group_2, slots_2.at[r], send_2.at[r], recv_2.at[r])
+        return measures(gather(group_2, slots_2.at[r], send_2.at[r], recv_2.at[r]))
+
+    def measures(row):
         total = jnp.sum(jnp.where(lane < 64, row, 0.0), axis=1, keepdims=True)
         product = jnp.sum(jnp.where(lane < 64, 0.0, row), axis=1, keepdims=True)
         inverse = 1.0 / jnp.sqrt(total / ENTRIES + EPSILON)
@@ -244,7 +248,7 @@
             for j in range(8):
                 keep = mask[chosen[b], i, j] > 0
                 tile = opv[chosen[b], rows, j * 128 : (j + 1) * 128]
-                a[b, rows, j * 128 : (j + 1) * 128] = jnp.where(keep, tile, jnp.zeros_like(tile))
+                a[b, j * 128 : (j + 1) * 128, rows] = jnp.where(keep, tile, jnp.zeros_like(tile)).T
 
     for b in range(4):
         mask_operator(b)
@@ -273,18 +277,12 @@
     def step(k, u, u_before, w, inverse, send=None):
         scale = jnp.broadcast_to(inverse, (8, LANES))
 
-        @pl.loop(0, 4)
-        def _(c):
-            cols = pl.ds(pl.multiple_of(c * 256, 256), 256)
-            here = u[:, cols]
-            total = None
-            for b in range(4):
-                product = lax.dot_general(
-                    ub[...], a[b, cols, :], (((1,), (1,)), ((), ())), preferred_element_type=F32
-                )
-                moved = flipped(product + fields[b] * here, b)
-                total = moved if total is None else total + moved
-            acc[:, cols] = total
+        total = None
+        for b in range(4):
+            product = jnp.dot(ub[...], a[b], preferred_element_type=F32)
+            moved = flipped(product + fields[b] * u[...], b)
+            total = moved if total is None else total + moved
+        acc[...] = total
 
         for copy in halo_copies(k, w):
             copy.wait_recv()
@@ -329,11 +327,11 @@
 
     normalize(r_in, u_0, inverse)
     squares, products = step(0, u_0, u_0, w_1, inverse)
-    scalars_start(1, "column", squares, products)
+    row = jnp.where(lane < 64, fold(squares), fold(products))
+    spread("whole", rows_1.at[1], slots_whole, row, send_1.at[1], recv_1.at[1])
     for copy in halo_copies(1, w_1):
         copy.start()
-    scalars_middle(1, "column", "layer")
-    inverse, moment = scalars_end(1, "layer")
+    inverse, moment = measures(gather("whole", slots_whole, send_1.at[1], recv_1.at[1]))
     set_moment(0, moment)
 
     normalize(w_1, u_1, inverse)
@@ -383,8 +381,11 @@
 
     for e in range(3):
         wait_send(t.at[pl.ds(0, 63 * 16), :], send_sem.at[e], recv_sem.at[e])
-    for r, (group, group_2) in enumerate(
-        (("plane", "line"), ("column", "layer"), ("column", "layer"), ("layer", "column"))
+    wait_send(slots_whole.at[pl.ds(0, 255)], send_1.at[1], recv_1.at[1])
+    for r, group, group_2 in (
+        (0, "plane", "line"),
+        (2, "column", "layer"),
+        (3, "layer", "column"),
     ):
         count, count_2 = groups[group][1], groups[group_2][1]
         wait_send(slots_1.at[r, pl.ds(0, count - 1)], send_1.at[r], recv_1.at[r])
@@ -435,6 +436,7 @@
             pltpu.VMEM((3, 2, 16, 8, LANES), F32),
             pltpu.VMEM((4, 64, 1, LANES), F32),
             pltpu.VMEM((4, 16, 1, LANES), F32),
+            pltpu.VMEM((256, 1, LANES), F32),
             pltpu.VMEM((4, 1, LANES), F32),
             pltpu.VMEM((4, 1, LANES), F32),
             flat,
@@ -452,7 +454,7 @@
             dma((4,)),
         ],
         compiler_params=pltpu.CompilerParams(
-            collective_id=0, has_side_effects=True, vmem_limit_bytes=48 * 1024 * 1024
+            collective_id=0, has_side_effects=True, vmem_limit_bytes=67043328
         ),
     )(state, operators, op_mask, site_bits, field, site_coupling, mode_coupling)
 

time: 81.1 us -> 75.5 us (0.931)
  Pallas kernels: 73.8 us -> 69.8 us
  local copies, waits for them, and re-layouts: 6.47 us -> 4.85 us
    pallas_call x1, Pallas kernels: 73.8 us -> 69.8 us  [shards(): pl.pallas_call(kernel, out_shape=(block, block, jax.ShapeDtypeStruct((STE...]
    unnamed x15 -> x3, local copies, waits for them, and re-layouts: 6.47 us -> 4.85 us
where the time goes in v3:
time: 75.5 us; the launch traced here: 75.3 us
  Pallas kernels  69.8 us (92%)
  local copies, waits for them, and re-layouts  4.85 us (6%)
    pallas_call x1, Pallas kernels, shards(): pl.pallas_call(kernel, out_shape=(block, block, jax.ShapeDtypeStruct((STE...  69.8 us
    unnamed x3, local copies, waits for them, and re-layouts  4.85 us

profile of v3, /device:TPU:1, one launch (start us, length us, event | category | flops | bytes accessed | tf_op | source)
XLA Modules:
  0.0 75.3 jit_solution(13974499157971580976)
XLA Ops:
  0.6 69.8 %shard_map.94 = (f32[1024,128]{1,0:T(8,128)}, f32[1024,128]{1,0:T(8,128)}, f32[3]{0:T(128)}) custom-call(f32[1024,128]{1,0:T(8,128)} %state.1, bf16[4,1024,1024]{2,1,0:T(8,128)(2,1)} %ops.1, s32[4,8,8]{2,1,0:T(8,128)} %mask_in.1, s32[4]{0:T(128)} %site_bits_in.1, f32[4]{0:T(128)} %field_in.1, f32[14]{0:T(128)} %site_coupling_in.1, f32[64]{0:T(128)} %mode_coupling_in.1), custom_call_target="tpu_custom_call" | custom-call | tf_op jit(solution)/shard_map/pallas_call | solution.py:409
  70.4 1.9 %copy.13 = f32[1024,128]{1,0:T(8,128)} copy(f32[1024,128]{1,0:T(8,128)} %get-tuple-element.6) | data formatting | bytes 1048576
  72.3 1.9 %copy.14 = f32[1024,128]{1,0:T(8,128)} copy(f32[1024,128]{1,0:T(8,128)} %get-tuple-element.7) | data formatting | bytes 1048576
  74.1 1.1 %copy.15 = f32[3]{0:T(128)} copy(f32[3]{0:T(128)} %get-tuple-element.8) | data formatting | bytes 24

commit v4 on v3

--- a/solution.py
+++ b/solution.py
@@ -50,11 +50,11 @@
 
 def kernel(
     state, ops, mask_in, site_bits_in, field_in, site_coupling_in, mode_coupling_in,
-    last, prev, moments,
+    r_3, r_2, stats,
     mask, site_bits, field, site_coupling, mode_coupling,
-    st, opv, a, t, r_in, r_2, r_3, w_1, w_2, w_3, u_0, u_1, u_2, ub, acc, occ, halo,
-    slots_1, slots_2, slots_whole, rows_1, rows_2, out_2, out_3,
-    load_sem, self_sem, out_sem, send_sem, recv_sem, hsend_sem, hrecv_sem,
+    st, opv, a, t, r_in, w_1, w_2, w_3, u_0, u_1, u_2, ub, acc, occ, halo,
+    slots_1, slots_2, slots_whole, rows_1, rows_2,
+    load_sem, self_sem, send_sem, recv_sem, hsend_sem, hrecv_sem,
     send_1, recv_1, send_2, recv_2,
 ):
     site = lax.axis_index("site")
@@ -314,16 +314,8 @@
 
         return lax.fori_loop(0, 16, body, (zero, zero))
 
-    def finish(r, inverse, out):
-        scale = jnp.broadcast_to(inverse, (128, LANES))
-        for high in range(8):
-            block = jnp.concatenate(
-                [r[pl.ds(high, 64, stride=16), :], r[pl.ds(8 + high, 64, stride=16), :]], axis=0
-            )
-            out[high * 128 : (high + 1) * 128, :] = block.T * scale
-
-    def set_moment(k, value):
-        moments[k] = value[0, 0]
+    def set_stat(k, value):
+        stats[k] = value[0, 0]
 
     normalize(r_in, u_0, inverse)
     squares, products = step(0, u_0, u_0, w_1, inverse)
@@ -332,7 +324,7 @@
     for copy in halo_copies(1, w_1):
         copy.start()
     inverse, moment = measures(gather("whole", slots_whole, send_1.at[1], recv_1.at[1]))
-    set_moment(0, moment)
+    set_stat(0, moment)
 
     normalize(w_1, u_1, inverse)
     squares, products = step(1, u_1, u_0, w_2, inverse)
@@ -342,8 +334,8 @@
     exchange_out_start(1, w_2, r_2)
     scalars_middle(2, "column", "layer")
     inverse, moment = scalars_end(2, "layer")
-    set_moment(1, moment)
-    inverse_2 = inverse
+    set_stat(1, moment)
+    set_stat(3, inverse)
 
     def send_ready(i):
         @pl.when(i > 0)
@@ -369,15 +361,10 @@
     scalars_start(3, "layer", squares, products)
     scalars_middle(3, "layer", "column")
     exchange_out_wait(1, w_2, r_2)
-    finish(r_2, inverse_2, out_2)
-    store_2 = pltpu.make_async_copy(out_2, prev, out_sem.at[0])
-    store_2.start()
     inverse, moment = scalars_end(3, "column")
-    set_moment(2, moment)
+    set_stat(2, moment)
+    set_stat(4, inverse)
     exchange_out_wait(2, w_3, r_3)
-    finish(r_3, inverse, out_3)
-    store_3 = pltpu.make_async_copy(out_3, last, out_sem.at[1])
-    store_3.start()
 
     for e in range(3):
         wait_send(t.at[pl.ds(0, 63 * 16), :], send_sem.at[e], recv_sem.at[e])
@@ -393,6 +380,37 @@
     for k, w in enumerate((r_in, w_1, w_2)):
         for copy in halo_copies(k, w):
             copy.wait_send()
+
+
+def finish_kernel(r_3, r_2, stats, last, prev, moments, v_3, v_2, out_3, out_2, held, kept, sem):
+    load = pltpu.make_async_copy(stats, held, sem.at[0])
+    load_2 = pltpu.make_async_copy(r_2, v_2, sem.at[1])
+    load_3 = pltpu.make_async_copy(r_3, v_3, sem.at[2])
+    load.start()
+    load_2.start()
+    load_3.start()
+
+    def finish(r, scale, out):
+        for high in range(8):
+            block = jnp.concatenate(
+                [r[pl.ds(high, 64, stride=16), :], r[pl.ds(8 + high, 64, stride=16), :]], axis=0
+            )
+            out[high * 128 : (high + 1) * 128, :] = block.T * scale
+
+    store = pltpu.make_async_copy(kept, moments, sem.at[3])
+    store_2 = pltpu.make_async_copy(out_2, prev, sem.at[4])
+    store_3 = pltpu.make_async_copy(out_3, last, sem.at[5])
+    load.wait()
+    for k in range(STEPS):
+        kept[k] = held[k]
+    store.start()
+    load_2.wait()
+    finish(v_2, held[3], out_2)
+    store_2.start()
+    load_3.wait()
+    finish(v_3, held[4], out_3)
+    store_3.start()
+    store.wait()
     store_2.wait()
     store_3.wait()
 
@@ -403,14 +421,13 @@
     cube = pltpu.VMEM((16, 64, LANES), F32)
     wide = pltpu.VMEM((LANES, ROWS), F32)
     dma = pltpu.SemaphoreType.DMA
-    anywhere = pl.BlockSpec(memory_space=pl.ANY)
     hbm = pl.BlockSpec(memory_space=pltpu.HBM)
     scalar = pl.BlockSpec(memory_space=pltpu.SMEM)
-    return pl.pallas_call(
+    carried = pl.pallas_call(
         kernel,
-        out_shape=(block, block, jax.ShapeDtypeStruct((STEPS,), F32)),
+        out_shape=(block, block, jax.ShapeDtypeStruct((8,), F32)),
         in_specs=[hbm] * 7,
-        out_specs=(anywhere, anywhere, scalar),
+        out_specs=(hbm, hbm, scalar),
         scratch_shapes=[
             pltpu.SMEM((4, 8, 8), jnp.int32),
             pltpu.SMEM((4,), jnp.int32),
@@ -422,8 +439,6 @@
             pltpu.VMEM((4, ROWS, ROWS), BF16),
             flat,
             cube,
-            flat,
-            flat,
             cube,
             cube,
             cube,
@@ -439,11 +454,8 @@
             pltpu.VMEM((256, 1, LANES), F32),
             pltpu.VMEM((4, 1, LANES), F32),
             pltpu.VMEM((4, 1, LANES), F32),
-            flat,
-            flat,
             dma((7,)),
             dma((3,)),
-            dma((2,)),
             dma((3,)),
             dma((3,)),
             dma((3, 2)),
@@ -457,6 +469,15 @@
             collective_id=0, has_side_effects=True, vmem_limit_bytes=67043328
         ),
     )(state, operators, op_mask, site_bits, field, site_coupling, mode_coupling)
+    return pl.pallas_call(
+        finish_kernel,
+        out_shape=(block, block, jax.ShapeDtypeStruct((STEPS,), F32)),
+        in_specs=[hbm] * 3,
+        out_specs=(hbm, hbm, hbm),
+        scratch_shapes=[flat] * 4
+        + [pltpu.SMEM((8,), F32), pltpu.SMEM((STEPS,), F32), dma((6,))],
+        compiler_params=pltpu.CompilerParams(vmem_limit_bytes=67043328),
+    )(*carried)
 
 
 def solution(mesh):

time: 75.5 us -> 71.8 us (0.951)
  local copies, waits for them, and re-layouts: 4.85 us -> 0 us
  Pallas kernels: 69.8 us -> 71.1 us
    unnamed x3 -> x0, local copies, waits for them, and re-layouts: 4.85 us -> none
    pallas_call x1 -> x2, Pallas kernels: 69.8 us -> 71.1 us  [the longest x1 68.8 us: shards(): pl.pallas_call(kernel, out_shape=(block, block, jax.ShapeDtypeStruct((8,)...]
where the time goes in v4:
time: 71.8 us; the launch traced here: 71.7 us
  Pallas kernels  71.1 us (99%)
    pallas_call x1, Pallas kernels, shards(): pl.pallas_call(kernel, out_shape=(block, block, jax.ShapeDtypeStruct((8,)...  68.8 us
    pallas_call x1, Pallas kernels, shards(): pl.pallas_call(finish_kernel, out_shape=(block, block, jax.ShapeDtypeStru...  2.32 us

profile of v4, /device:TPU:1, one launch (start us, length us, event | category | flops | bytes accessed | tf_op | source)
XLA Modules:
  0.0 71.7 jit_solution(18307253246352574005)
XLA Ops:
  0.6 68.8 %shard_map.94 = (f32[1024,128]{1,0:T(8,128)}, f32[1024,128]{1,0:T(8,128)}, f32[8]{0:T(128)}) custom-call(f32[1024,128]{1,0:T(8,128)} %state.1, bf16[4,1024,1024]{2,1,0:T(8,128)(2,1)} %ops.1, s32[4,8,8]{2,1,0:T(8,128)} %mask_in.1, s32[4]{0:T(128)} %site_bits_in.1, f32[4]{0:T(128)} %field_in.1, f32[14]{0:T(128)} %site_coupling_in.1, f32[64]{0:T(128)} %mode_coupling_in.1), custom_call_target="tpu_custom_call" | custom-call | tf_op jit(solution)/shard_map/pallas_call | solution.py:426
  69.4 2.3 %shard_map.95 = (f32[1024,128]{1,0:T(8,128)}, f32[1024,128]{1,0:T(8,128)}, f32[3]{0:T(128)}) custom-call(f32[1024,128]{1,0:T(8,128)} %get-tuple-element.6.r_3, f32[1024,128]{1,0:T(8,128)} %get-tuple-element.7.r_2, f32[8]{0:T(128)} %get-tuple-element.8.stats), custom_call_target="tpu_custom_call" | custom-call | tf_op jit(solution)/shard_map/pallas_call | solution.py:472

commit v5 on v4

--- a/solution.py
+++ b/solution.py
@@ -52,9 +52,9 @@
     state, ops, mask_in, site_bits_in, field_in, site_coupling_in, mode_coupling_in,
     r_3, r_2, stats,
     mask, site_bits, field, site_coupling, mode_coupling,
-    st, opv, a, t, r_in, w_1, w_2, w_3, u_0, u_1, u_2, ub, acc, occ, halo,
+    st, opv, a, t, r_in, w_1, w_2, w_3, u_0, u_1, ub, acc, linear, occ, halo,
     slots_1, slots_2, slots_whole, rows_1, rows_2,
-    load_sem, self_sem, send_sem, recv_sem, hsend_sem, hrecv_sem,
+    load_sem, self_sem, in_sem, send_sem, recv_sem, hsend_sem, hrecv_sem,
     send_1, recv_1, send_2, recv_2,
 ):
     site = lax.axis_index("site")
@@ -171,22 +171,21 @@
     def chunk3(ref, site_at, q_at):
         return ref.at[site_at, pl.ds(pl.multiple_of(q_at * 16, 16), 16), :]
 
-    def exchange_in_self():
-        return pltpu.make_async_copy(chunk2(t, mode), chunk3(r_in, site, q), self_sem.at[0])
+    early = (q == 0) | (q == 3)
+    kind = jnp.where(early, 0, 1)
 
     def exchange_in_start():
-        exchange_in_self().start()
+        pltpu.make_async_copy(chunk2(t, mode), chunk3(r_in, site, q), in_sem.at[kind]).start()
         for offset in PLANE:
             site_at, y_at, q_at = place_of(offset)
             pltpu.make_async_remote_copy(
                 src_ref=chunk2(t, site_at * 4 + q_at), dst_ref=chunk3(r_in, site, q),
-                send_sem=send_sem.at[0], recv_sem=recv_sem.at[0],
+                send_sem=send_sem.at[0], recv_sem=in_sem.at[kind],
                 device_id=(site_at, y_at * 4 + q_at), device_id_type=MESH,
             ).start()
 
-    def exchange_in_wait():
-        exchange_in_self().wait()
-        wait_recv(t.at[pl.ds(0, 63 * 16), :], send_sem.at[0], recv_sem.at[0])
+    def exchange_in_wait(which):
+        wait_recv(t.at[pl.ds(0, 32 * 16), :], send_sem.at[0], in_sem.at[which])
 
     def exchange_out_self(e, w, r):
         return pltpu.make_async_copy(chunk3(w, site, q), chunk2(r, mode), self_sem.at[e])
@@ -220,7 +219,7 @@
 
     pl.semaphore_wait(barrier, 66)
     scalars_start(0, "plane", squares, zero)
-    exchange_in_start()
+    pl.when(early)(exchange_in_start)
 
     for copy in small:
         copy.wait()
@@ -252,10 +251,12 @@
 
     for b in range(4):
         mask_operator(b)
+    pl.when(jnp.logical_not(early))(exchange_in_start)
     scalars_middle(0, "plane", "line")
-    exchange_in_wait()
+    exchange_in_wait(0)
     for copy in halo_copies(0, r_in):
         copy.start()
+    exchange_in_wait(1)
     inverse, _ = scalars_end(0, "line")
 
     sublane = lax.broadcasted_iota(jnp.int32, (8, LANES), 0)
@@ -271,38 +272,58 @@
                 second = w[2 * e + 1, pl.ds(high, 8, stride=8), :] * scale
                 both = jnp.concatenate([first, second], axis=0)
                 rows = pl.ds(pl.multiple_of(e * 16, 16), 16)
-                u[rows, cols] = both
+                if u is not None:
+                    u[rows, cols] = both
                 ub[rows, cols] = both.astype(BF16)
 
-    def step(k, u, u_before, w, inverse, send=None):
-        scale = jnp.broadcast_to(inverse, (8, LANES))
-
+    def bits_of(d):
+        return [(d // (1 << b)) % 2 for b in range(4)]
+
+    def ladder_of(k, d, high, here):
+        cols = slice(high * 128, (high + 1) * 128)
+        constant = F32(0.0)
+        for b, bit in enumerate(bits_of(d)):
+            constant = constant + device_coupling[b] * bit.astype(F32)
+        below = jnp.broadcast_to(halo[k, 0, d, high : high + 1, :], (8, LANES))
+        above = jnp.broadcast_to(halo[k, 1, d, high : high + 1, :], (8, LANES))
+        lower = jnp.where(sublane == 0, below, pltpu.roll(here, 1, 0))
+        upper = jnp.where(sublane == 7, above, pltpu.roll(here, 7, 0))
+        return (occ[:, cols] + constant) * (lower_weight * lower + upper_weight * upper)
+
+    def prepare(k, w_before, w):
+        for copy in halo_copies(k, w):
+            copy.wait_recv()
+
+        @pl.loop(0, 16)
+        def _(d):
+            bits = bits_of(d)
+            rows = pl.ds(pl.multiple_of(d * 8, 8), 8)
+            for high in range(8):
+                cols = slice(high * 128, (high + 1) * 128)
+                here = w_before[d, pl.ds(high, 8, stride=8), :]
+                value = ladder_of(k, d, high, here)
+                for b in range(4):
+                    other = d + (1 - 2 * bits[b]) * (1 << b)
+                    value = value + fields[b] * w_before[other, pl.ds(high, 8, stride=8), :]
+                linear[rows, cols] = value
+
+    def multiply():
         total = None
         for b in range(4):
-            product = jnp.dot(ub[...], a[b], preferred_element_type=F32)
-            moved = flipped(product + fields[b] * u[...], b)
-            total = moved if total is None else total + moved
+            product = flipped(jnp.dot(ub[...], a[b], preferred_element_type=F32), b)
+            total = product if total is None else total + product
         acc[...] = total
 
-        for copy in halo_copies(k, w):
-            copy.wait_recv()
+    def combine(k, u_before, w, inverse, send=None):
+        scale = jnp.broadcast_to(inverse, (8, LANES))
 
         def body(i, carry):
             squares, products = carry
             d = (site + 1 + i) % 16
-            constant = F32(0.0)
-            for b in range(4):
-                constant = constant + device_coupling[b] * ((d >> b) & 1).astype(F32)
             rows = pl.ds(pl.multiple_of(d * 8, 8), 8)
             for high in range(8):
                 cols = slice(high * 128, (high + 1) * 128)
-                here = u[rows, cols]
-                below = jnp.broadcast_to(halo[k, 0, d, high : high + 1, :], (8, LANES)) * scale
-                above = jnp.broadcast_to(halo[k, 1, d, high : high + 1, :], (8, LANES)) * scale
-                lower = jnp.where(sublane == 0, below, pltpu.roll(here, 1, 0))
-                upper = jnp.where(sublane == 7, above, pltpu.roll(here, 7, 0))
-                ladder = (occ[:, cols] + constant) * (lower_weight * lower + upper_weight * upper)
-                new = acc[rows, cols] + ladder
+                new = acc[rows, cols] + linear[rows, cols] * scale
                 if k > 0:
                     new = 2.0 * new - u_before[rows, cols] * scale
                 w[d, pl.ds(high, 8, stride=8), :] = new
@@ -318,20 +339,25 @@
         stats[k] = value[0, 0]
 
     normalize(r_in, u_0, inverse)
-    squares, products = step(0, u_0, u_0, w_1, inverse)
+    multiply()
+    prepare(0, r_in, w_1)
+    squares, products = combine(0, None, w_1, inverse)
     row = jnp.where(lane < 64, fold(squares), fold(products))
     spread("whole", rows_1.at[1], slots_whole, row, send_1.at[1], recv_1.at[1])
     for copy in halo_copies(1, w_1):
         copy.start()
+    prepare(1, w_1, w_2)
     inverse, moment = measures(gather("whole", slots_whole, send_1.at[1], recv_1.at[1]))
     set_stat(0, moment)
 
     normalize(w_1, u_1, inverse)
-    squares, products = step(1, u_1, u_0, w_2, inverse)
+    multiply()
+    squares, products = combine(1, u_0, w_2, inverse)
     scalars_start(2, "column", squares, products)
     for copy in halo_copies(2, w_2):
         copy.start()
     exchange_out_start(1, w_2, r_2)
+    prepare(2, w_2, w_3)
     scalars_middle(2, "column", "layer")
     inverse, moment = scalars_end(2, "layer")
     set_stat(1, moment)
@@ -348,8 +374,9 @@
                     device_id=(d, y * 4 + q_at), device_id_type=MESH,
                 ).start()
 
-    normalize(w_2, u_2, inverse)
-    squares, products = step(2, u_2, u_1, w_3, inverse, send_ready)
+    normalize(w_2, None, inverse)
+    multiply()
+    squares, products = combine(2, u_1, w_3, inverse, send_ready)
     for j in range(1, 4):
         q_at = (q + j) % 4
         pltpu.make_async_remote_copy(
@@ -382,7 +409,7 @@
             copy.wait_send()
 
 
-def finish_kernel(r_3, r_2, stats, last, prev, moments, v_3, v_2, out_3, out_2, held, kept, sem):
+def finish_kernel(r_3, r_2, stats, last, prev, moments, v_3, v_2, out_3, out_2, held, kept, sem, store_sem):
     load = pltpu.make_async_copy(stats, held, sem.at[0])
     load_2 = pltpu.make_async_copy(r_2, v_2, sem.at[1])
     load_3 = pltpu.make_async_copy(r_3, v_3, sem.at[2])
@@ -390,29 +417,36 @@
     load_2.start()
     load_3.start()
 
-    def finish(r, scale, out):
+    def finish(r, scale, out, stores):
         for high in range(8):
             block = jnp.concatenate(
                 [r[pl.ds(high, 64, stride=16), :], r[pl.ds(8 + high, 64, stride=16), :]], axis=0
             )
             out[high * 128 : (high + 1) * 128, :] = block.T * scale
+            stores[high].start()
+
+    def stores_of(out, result, k):
+        return [
+            pltpu.make_async_copy(
+                out.at[pl.ds(high * 128, 128), :], result.at[pl.ds(high * 128, 128), :], store_sem.at[k, high]
+            )
+            for high in range(8)
+        ]
 
     store = pltpu.make_async_copy(kept, moments, sem.at[3])
-    store_2 = pltpu.make_async_copy(out_2, prev, sem.at[4])
-    store_3 = pltpu.make_async_copy(out_3, last, sem.at[5])
+    stores_2 = stores_of(out_2, prev, 0)
+    stores_3 = stores_of(out_3, last, 1)
     load.wait()
     for k in range(STEPS):
         kept[k] = held[k]
     store.start()
     load_2.wait()
-    finish(v_2, held[3], out_2)
-    store_2.start()
+    finish(v_2, held[3], out_2, stores_2)
     load_3.wait()
-    finish(v_3, held[4], out_3)
-    store_3.start()
+    finish(v_3, held[4], out_3, stores_3)
     store.wait()
-    store_2.wait()
-    store_3.wait()
+    for copy in stores_2 + stores_3:
+        copy.wait()
 
 
 def shards(state, operators, op_mask, site_bits, field, site_coupling, mode_coupling):
@@ -444,8 +478,8 @@
             cube,
             wide,
             wide,
+            pltpu.VMEM((LANES, ROWS), BF16),
             wide,
-            pltpu.VMEM((LANES, ROWS), BF16),
             wide,
             pltpu.VMEM((8, ROWS), F32),
             pltpu.VMEM((3, 2, 16, 8, LANES), F32),
@@ -456,6 +490,7 @@
             pltpu.VMEM((4, 1, LANES), F32),
             dma((7,)),
             dma((3,)),
+            dma((2,)),
             dma((3,)),
             dma((3,)),
             dma((3, 2)),
@@ -475,7 +510,7 @@
         in_specs=[hbm] * 3,
         out_specs=(hbm, hbm, hbm),
         scratch_shapes=[flat] * 4
-        + [pltpu.SMEM((8,), F32), pltpu.SMEM((STEPS,), F32), dma((6,))],
+        + [pltpu.SMEM((8,), F32), pltpu.SMEM((STEPS,), F32), dma((4,)), dma((2, 8))],
         compiler_params=pltpu.CompilerParams(vmem_limit_bytes=67043328),
     )(*carried)
 

time: 71.8 us -> 70.6 us (0.983)
  Pallas kernels: 71.1 us -> 69.8 us
    pallas_call x1, Pallas kernels: 68.8 us -> 67.5 us  [shards(): pl.pallas_call(kernel, out_shape=(block, block, jax.ShapeDtypeStruct((8,)...]
where the time goes in v5:
time: 70.6 us; the launch traced here: 70.5 us
  Pallas kernels  69.8 us (99%)
    pallas_call x1, Pallas kernels, shards(): pl.pallas_call(kernel, out_shape=(block, block, jax.ShapeDtypeStruct((8,)...  67.5 us
    pallas_call x1, Pallas kernels, shards(): pl.pallas_call(finish_kernel, out_shape=(block, block, jax.ShapeDtypeStru...  2.32 us

profile of v5, /device:TPU:1, one launch (start us, length us, event | category | flops | bytes accessed | tf_op | source)
XLA Modules:
  0.0 70.5 jit_solution(10147307813918335914)
XLA Ops:
  0.6 67.5 %shard_map.94 = (f32[1024,128]{1,0:T(8,128)}, f32[1024,128]{1,0:T(8,128)}, f32[8]{0:T(128)}) custom-call(f32[1024,128]{1,0:T(8,128)} %state.1, bf16[4,1024,1024]{2,1,0:T(8,128)(2,1)} %ops.1, s32[4,8,8]{2,1,0:T(8,128)} %mask_in.1, s32[4]{0:T(128)} %site_bits_in.1, f32[4]{0:T(128)} %field_in.1, f32[14]{0:T(128)} %site_coupling_in.1, f32[64]{0:T(128)} %mode_coupling_in.1), custom_call_target="tpu_custom_call" | custom-call | tf_op jit(solution)/shard_map/pallas_call | solution.py:460
  68.1 2.3 %shard_map.95 = (f32[1024,128]{1,0:T(8,128)}, f32[1024,128]{1,0:T(8,128)}, f32[3]{0:T(128)}) custom-call(f32[1024,128]{1,0:T(8,128)} %get-tuple-element.6.r_3, f32[1024,128]{1,0:T(8,128)} %get-tuple-element.7.r_2, f32[8]{0:T(128)} %get-tuple-element.8.stats), custom_call_target="tpu_custom_call" | custom-call | tf_op jit(solution)/shard_map/pallas_call | solution.py:507

commit v6 on v5

--- a/solution.py
+++ b/solution.py
@@ -277,6 +277,8 @@
                 ub[rows, cols] = both.astype(BF16)
 
     def bits_of(d):
+        if isinstance(d, int):
+            return [jnp.int32((d >> b) & 1) for b in range(4)]
         return [(d // (1 << b)) % 2 for b in range(4)]
 
     def ladder_of(k, d, high, here):
@@ -306,6 +308,31 @@
                     other = d + (1 - 2 * bits[b]) * (1 << b)
                     value = value + fields[b] * w_before[other, pl.ds(high, 8, stride=8), :]
                 linear[rows, cols] = value
+
+    def linear_part(w_before, k, d, high):
+        value = ladder_of(k, d, high, w_before[d, pl.ds(high, 8, stride=8), :])
+        for b in range(4):
+            value = value + fields[b] * w_before[d ^ (1 << b), pl.ds(high, 8, stride=8), :]
+        return value
+
+    def step(k, u_before, w_before, w, inverse, part):
+        scale = jnp.broadcast_to(inverse, (8, LANES))
+        total = None
+        for b in range(4):
+            product = flipped(jnp.dot(ub[...], a[b], preferred_element_type=F32), b)
+            total = product if total is None else total + product
+        squares, products = zero, zero
+        for d in range(16):
+            rows = slice(d * 8, (d + 1) * 8)
+            for high in range(8):
+                cols = slice(high * 128, (high + 1) * 128)
+                new = total[rows, cols] + part(d, high) * scale
+                if k > 0:
+                    new = 2.0 * new - u_before[rows, cols] * scale
+                w[d, pl.ds(high, 8, stride=8), :] = new
+                squares = squares + new * new
+                products = products + u_0[rows, cols] * new
+        return squares, products
 
     def multiply():
         total = None
@@ -339,9 +366,11 @@
         stats[k] = value[0, 0]
 
     normalize(r_in, u_0, inverse)
-    multiply()
-    prepare(0, r_in, w_1)
-    squares, products = combine(0, None, w_1, inverse)
+    for copy in halo_copies(0, r_in):
+        copy.wait_recv()
+    squares, products = step(
+        0, None, r_in, w_1, inverse, lambda d, high: linear_part(r_in, 0, d, high)
+    )
     row = jnp.where(lane < 64, fold(squares), fold(products))
     spread("whole", rows_1.at[1], slots_whole, row, send_1.at[1], recv_1.at[1])
     for copy in halo_copies(1, w_1):
@@ -351,8 +380,10 @@
     set_stat(0, moment)
 
     normalize(w_1, u_1, inverse)
-    multiply()
-    squares, products = combine(1, u_0, w_2, inverse)
+    squares, products = step(
+        1, u_0, w_1, w_2, inverse,
+        lambda d, high: linear[d * 8 : (d + 1) * 8, high * 128 : (high + 1) * 128],
+    )
     scalars_start(2, "column", squares, products)
     for copy in halo_copies(2, w_2):
         copy.start()
@@ -363,32 +394,16 @@
     set_stat(1, moment)
     set_stat(3, inverse)
 
-    def send_ready(i):
-        @pl.when(i > 0)
-        def _():
-            d = (site + i) % 16
-            for q_at in range(4):
-                pltpu.make_async_remote_copy(
-                    src_ref=chunk3(w_3, d, q_at), dst_ref=chunk2(r_3, mode),
-                    send_sem=send_sem.at[2], recv_sem=recv_sem.at[2],
-                    device_id=(d, y * 4 + q_at), device_id_type=MESH,
-                ).start()
-
     normalize(w_2, None, inverse)
-    multiply()
-    squares, products = combine(2, u_1, w_3, inverse, send_ready)
-    for j in range(1, 4):
-        q_at = (q + j) % 4
-        pltpu.make_async_remote_copy(
-            src_ref=chunk3(w_3, site, q_at), dst_ref=chunk2(r_3, mode),
-            send_sem=send_sem.at[2], recv_sem=recv_sem.at[2],
-            device_id=(site, y * 4 + q_at), device_id_type=MESH,
-        ).start()
-    exchange_out_self(2, w_3, r_3).start()
-    scalars_start(3, "layer", squares, products)
-    scalars_middle(3, "layer", "column")
+    squares, products = step(
+        2, u_1, w_2, w_3, inverse,
+        lambda d, high: linear[d * 8 : (d + 1) * 8, high * 128 : (high + 1) * 128],
+    )
+    scalars_start(3, "column", squares, products)
+    exchange_out_start(2, w_3, r_3)
+    scalars_middle(3, "column", "layer")
     exchange_out_wait(1, w_2, r_2)
-    inverse, moment = scalars_end(3, "column")
+    inverse, moment = scalars_end(3, "layer")
     set_stat(2, moment)
     set_stat(4, inverse)
     exchange_out_wait(2, w_3, r_3)
@@ -399,7 +414,7 @@
     for r, group, group_2 in (
         (0, "plane", "line"),
         (2, "column", "layer"),
-        (3, "layer", "column"),
+        (3, "column", "layer"),
     ):
         count, count_2 = groups[group][1], groups[group_2][1]
         wait_send(slots_1.at[r, pl.ds(0, count - 1)], send_1.at[r], recv_1.at[r])

time: 70.6 us -> 69.7 us (0.987)
  Pallas kernels: 69.8 us -> 69 us
    pallas_call x1, Pallas kernels: 67.5 us -> 66.7 us  [shards(): pl.pallas_call(kernel, out_shape=(block, block, jax.ShapeDtypeStruct((8,)...]
where the time goes in v6:
time: 69.7 us; the launch traced here: 69.6 us
  Pallas kernels  69 us (99%)
    pallas_call x1, Pallas kernels, shards(): pl.pallas_call(kernel, out_shape=(block, block, jax.ShapeDtypeStruct((8,)...  66.7 us
    pallas_call x1, Pallas kernels, shards(): pl.pallas_call(finish_kernel, out_shape=(block, block, jax.ShapeDtypeStru...  2.32 us

profile of v6, /device:TPU:1, one launch (start us, length us, event | category | flops | bytes accessed | tf_op | source)
XLA Modules:
  0.0 69.6 jit_solution(17468485889489033169)
XLA Ops:
  0.6 66.7 %shard_map.94 = (f32[1024,128]{1,0:T(8,128)}, f32[1024,128]{1,0:T(8,128)}, f32[8]{0:T(128)}) custom-call(f32[1024,128]{1,0:T(8,128)} %state.1, bf16[4,1024,1024]{2,1,0:T(8,128)(2,1)} %ops.1, s32[4,8,8]{2,1,0:T(8,128)} %mask_in.1, s32[4]{0:T(128)} %site_bits_in.1, f32[4]{0:T(128)} %field_in.1, f32[14]{0:T(128)} %site_coupling_in.1, f32[64]{0:T(128)} %mode_coupling_in.1), custom_call_target="tpu_custom_call" | custom-call | tf_op jit(solution)/shard_map/pallas_call | solution.py:475
  67.3 2.3 %shard_map.95 = (f32[1024,128]{1,0:T(8,128)}, f32[1024,128]{1,0:T(8,128)}, f32[3]{0:T(128)}) custom-call(f32[1024,128]{1,0:T(8,128)} %get-tuple-element.6.r_3, f32[1024,128]{1,0:T(8,128)} %get-tuple-element.7.r_2, f32[8]{0:T(128)} %get-tuple-element.8.stats), custom_call_target="tpu_custom_call" | custom-call | tf_op jit(solution)/shard_map/pallas_call | solution.py:522

commit v7 on v6

--- a/solution.py
+++ b/solution.py
@@ -45,16 +45,23 @@
 LINE = offsets(ys=4)
 COLUMN = offsets(zs=8, cores=2)
 LAYER = offsets(xs=4, ys=4)
+ROW = offsets(xs=4)
 WHOLE = offsets(zs=8, xs=4, ys=4, cores=2)
+
+
+def finished(r, high):
+    lower = r[pl.ds(high, 64, stride=16), :]
+    upper = r[pl.ds(8 + high, 64, stride=16), :]
+    return jnp.concatenate([lower, upper], axis=0).T
 
 
 def kernel(
     state, ops, mask_in, site_bits_in, field_in, site_coupling_in, mode_coupling_in,
-    r_3, r_2, stats,
+    r_3, ready, stats,
     mask, site_bits, field, site_coupling, mode_coupling,
-    st, opv, a, t, r_in, w_1, w_2, w_3, u_0, u_1, ub, acc, linear, occ, halo,
+    st, opv, a, t, r_in, r_2, out_2, w_1, w_2, w_3, u_0, u_1, ub, acc, linear, occ, halo,
     slots_1, slots_2, slots_whole, rows_1, rows_2,
-    load_sem, self_sem, in_sem, send_sem, recv_sem, hsend_sem, hrecv_sem,
+    load_sem, self_sem, in_sem, line_sem, out_sem, send_sem, recv_sem, hsend_sem, hrecv_sem,
     send_1, recv_1, send_2, recv_2,
 ):
     site = lax.axis_index("site")
@@ -126,8 +133,8 @@
         ).wait_send()
 
     groups = {
-        "plane": (PLANE, 64, site * 4 + q),
         "line": (LINE, 4, y),
+        "row": (ROW, 4, x),
         "column": (COLUMN, 16, z * 2 + core),
         "layer": (LAYER, 16, x * 4 + y),
         "whole": (WHOLE, 256, site * 16 + phonon),
@@ -146,7 +153,12 @@
     def gather(group, slots, send, recv):
         members, count, index = groups[group]
         wait_recv(slots.at[pl.ds(0, count - 1)], send, recv)
-        return jnp.sum(slots[0:count], axis=0)
+        if count <= 16:
+            return jnp.sum(slots[0:count], axis=0)
+        value = slots[0:8]
+        for i in range(8, count, 8):
+            value = value + slots[i : i + 8]
+        return jnp.sum(value, axis=0)
 
     def scalars_start(r, group, squares, products):
         row = jnp.where(lane < 64, fold(squares), fold(products))
@@ -218,7 +230,7 @@
         return up, down
 
     pl.semaphore_wait(barrier, 66)
-    scalars_start(0, "plane", squares, zero)
+    scalars_start(0, "column", squares, zero)
     pl.when(early)(exchange_in_start)
 
     for copy in small:
@@ -252,12 +264,14 @@
     for b in range(4):
         mask_operator(b)
     pl.when(jnp.logical_not(early))(exchange_in_start)
-    scalars_middle(0, "plane", "line")
+    scalars_middle(0, "column", "row")
+    row = gather("row", slots_2.at[0], send_2.at[0], recv_2.at[0])
+    spread("line", rows_1.at[1], slots_1.at[1], row, line_sem.at[0], line_sem.at[1])
     exchange_in_wait(0)
     for copy in halo_copies(0, r_in):
         copy.start()
     exchange_in_wait(1)
-    inverse, _ = scalars_end(0, "line")
+    inverse, _ = measures(gather("line", slots_1.at[1], line_sem.at[0], line_sem.at[1]))
 
     sublane = lax.broadcasted_iota(jnp.int32, (8, LANES), 0)
 
@@ -372,7 +386,7 @@
         0, None, r_in, w_1, inverse, lambda d, high: linear_part(r_in, 0, d, high)
     )
     row = jnp.where(lane < 64, fold(squares), fold(products))
-    spread("whole", rows_1.at[1], slots_whole, row, send_1.at[1], recv_1.at[1])
+    spread("whole", rows_2.at[1], slots_whole, row, send_1.at[1], recv_1.at[1])
     for copy in halo_copies(1, w_1):
         copy.start()
     prepare(1, w_1, w_2)
@@ -392,7 +406,7 @@
     scalars_middle(2, "column", "layer")
     inverse, moment = scalars_end(2, "layer")
     set_stat(1, moment)
-    set_stat(3, inverse)
+    inverse_2 = inverse
 
     normalize(w_2, None, inverse)
     squares, products = step(
@@ -403,16 +417,23 @@
     exchange_out_start(2, w_3, r_3)
     scalars_middle(3, "column", "layer")
     exchange_out_wait(1, w_2, r_2)
+    scale_2 = jnp.broadcast_to(inverse_2, (128, LANES))
+    for high in range(8):
+        out_2[high * 128 : (high + 1) * 128, :] = finished(r_2, high) * scale_2
+    store_2 = pltpu.make_async_copy(out_2, ready, out_sem)
+    store_2.start()
     inverse, moment = scalars_end(3, "layer")
     set_stat(2, moment)
-    set_stat(4, inverse)
+    set_stat(3, inverse)
     exchange_out_wait(2, w_3, r_3)
+    store_2.wait()
 
     for e in range(3):
         wait_send(t.at[pl.ds(0, 63 * 16), :], send_sem.at[e], recv_sem.at[e])
+    wait_send(slots_1.at[1, pl.ds(0, 3)], line_sem.at[0], line_sem.at[1])
     wait_send(slots_whole.at[pl.ds(0, 255)], send_1.at[1], recv_1.at[1])
     for r, group, group_2 in (
-        (0, "plane", "line"),
+        (0, "column", "row"),
         (2, "column", "layer"),
         (3, "column", "layer"),
     ):
@@ -424,43 +445,31 @@
             copy.wait_send()
 
 
-def finish_kernel(r_3, r_2, stats, last, prev, moments, v_3, v_2, out_3, out_2, held, kept, sem, store_sem):
+def finish_kernel(r_3, ready, stats, last, prev, moments, v_3, v_2, out_3, held, kept, sem, store_sem):
     load = pltpu.make_async_copy(stats, held, sem.at[0])
-    load_2 = pltpu.make_async_copy(r_2, v_2, sem.at[1])
-    load_3 = pltpu.make_async_copy(r_3, v_3, sem.at[2])
+    load_3 = pltpu.make_async_copy(r_3, v_3, sem.at[1])
+    load_2 = pltpu.make_async_copy(ready, v_2, sem.at[2])
+    store = pltpu.make_async_copy(kept, moments, sem.at[3])
+    store_2 = pltpu.make_async_copy(v_2, prev, sem.at[4])
     load.start()
+    load_3.start()
     load_2.start()
-    load_3.start()
-
-    def finish(r, scale, out, stores):
-        for high in range(8):
-            block = jnp.concatenate(
-                [r[pl.ds(high, 64, stride=16), :], r[pl.ds(8 + high, 64, stride=16), :]], axis=0
-            )
-            out[high * 128 : (high + 1) * 128, :] = block.T * scale
-            stores[high].start()
-
-    def stores_of(out, result, k):
-        return [
-            pltpu.make_async_copy(
-                out.at[pl.ds(high * 128, 128), :], result.at[pl.ds(high * 128, 128), :], store_sem.at[k, high]
-            )
-            for high in range(8)
-        ]
-
-    store = pltpu.make_async_copy(kept, moments, sem.at[3])
-    stores_2 = stores_of(out_2, prev, 0)
-    stores_3 = stores_of(out_3, last, 1)
     load.wait()
     for k in range(STEPS):
         kept[k] = held[k]
     store.start()
-    load_2.wait()
-    finish(v_2, held[3], out_2, stores_2)
     load_3.wait()
-    finish(v_3, held[4], out_3, stores_3)
-    store.wait()
-    for copy in stores_2 + stores_3:
+    scale = held[3]
+    stores = []
+    for high in range(8):
+        rows = pl.ds(high * 128, 128)
+        out_3[rows, :] = finished(v_3, high) * scale
+        stores.append(pltpu.make_async_copy(out_3.at[rows, :], last.at[rows, :], store_sem.at[high]))
+        stores[high].start()
+        if high == 0:
+            load_2.wait()
+            store_2.start()
+    for copy in stores + [store, store_2]:
         copy.wait()
 
 
@@ -488,6 +497,8 @@
             pltpu.VMEM((4, ROWS, ROWS), BF16),
             flat,
             cube,
+            flat,
+            flat,
             cube,
             cube,
             cube,
@@ -498,7 +509,7 @@
             wide,
             pltpu.VMEM((8, ROWS), F32),
             pltpu.VMEM((3, 2, 16, 8, LANES), F32),
-            pltpu.VMEM((4, 64, 1, LANES), F32),
+            pltpu.VMEM((4, 16, 1, LANES), F32),
             pltpu.VMEM((4, 16, 1, LANES), F32),
             pltpu.VMEM((256, 1, LANES), F32),
             pltpu.VMEM((4, 1, LANES), F32),
@@ -506,6 +517,8 @@
             dma((7,)),
             dma((3,)),
             dma((2,)),
+            dma((2,)),
+            dma,
             dma((3,)),
             dma((3,)),
             dma((3, 2)),
@@ -524,8 +537,8 @@
         out_shape=(block, block, jax.ShapeDtypeStruct((STEPS,), F32)),
         in_specs=[hbm] * 3,
         out_specs=(hbm, hbm, hbm),
-        scratch_shapes=[flat] * 4
-        + [pltpu.SMEM((8,), F32), pltpu.SMEM((STEPS,), F32), dma((4,)), dma((2, 8))],
+        scratch_shapes=[flat] * 3
+        + [pltpu.SMEM((8,), F32), pltpu.SMEM((STEPS,), F32), dma((5,)), dma((8,))],
         compiler_params=pltpu.CompilerParams(vmem_limit_bytes=67043328),
     )(*carried)
 

time: 69.7 us -> 68.9 us (0.989)
  Pallas kernels: 69 us -> 68.1 us
    pallas_call x1, Pallas kernels: 66.7 us -> 65.9 us  [shards(): pl.pallas_call(kernel, out_shape=(block, block, jax.ShapeDtypeStruct((8,)...]
where the time goes in v7:
time: 68.9 us; the launch traced here: 68.8 us
  Pallas kernels  68.1 us (99%)
    pallas_call x1, Pallas kernels, shards(): pl.pallas_call(kernel, out_shape=(block, block, jax.ShapeDtypeStruct((8,)...  65.9 us
    pallas_call x1, Pallas kernels, shards(): pl.pallas_call(finish_kernel, out_shape=(block, block, jax.ShapeDtypeStru...  2.25 us

profile of v7, /device:TPU:1, one launch (start us, length us, event | category | flops | bytes accessed | tf_op | source)
XLA Modules:
  0.0 68.8 jit_solution(1037106228532133485)
XLA Ops:
  0.6 65.9 %shard_map.94 = (f32[1024,128]{1,0:T(8,128)}, f32[1024,128]{1,0:T(8,128)}, f32[8]{0:T(128)}) custom-call(f32[1024,128]{1,0:T(8,128)} %state.1, bf16[4,1024,1024]{2,1,0:T(8,128)(2,1)} %ops.1, s32[4,8,8]{2,1,0:T(8,128)} %mask_in.1, s32[4]{0:T(128)} %site_bits_in.1, f32[4]{0:T(128)} %field_in.1, f32[14]{0:T(128)} %site_coupling_in.1, f32[64]{0:T(128)} %mode_coupling_in.1), custom_call_target="tpu_custom_call" | custom-call | tf_op jit(solution)/shard_map/pallas_call | solution.py:484
  66.5 2.3 %shard_map.95 = (f32[1024,128]{1,0:T(8,128)}, f32[1024,128]{1,0:T(8,128)}, f32[3]{0:T(128)}) custom-call(f32[1024,128]{1,0:T(8,128)} %get-tuple-element.6.r_3, f32[1024,128]{1,0:T(8,128)} %get-tuple-element.7.ready, f32[8]{0:T(128)} %get-tuple-element.8.stats), custom_call_target="tpu_custom_call" | custom-call | tf_op jit(solution)/shard_map/pallas_call | solution.py:535

commit v8 on v7

--- a/solution.py
+++ b/solution.py
@@ -295,16 +295,22 @@
             return [jnp.int32((d >> b) & 1) for b in range(4)]
         return [(d // (1 << b)) % 2 for b in range(4)]
 
-    def ladder_of(k, d, high, here):
-        cols = slice(high * 128, (high + 1) * 128)
+    def occupancy(d, high):
         constant = F32(0.0)
         for b, bit in enumerate(bits_of(d)):
             constant = constant + device_coupling[b] * bit.astype(F32)
+        return occ[:, high * 128 : (high + 1) * 128] + constant
+
+    def halo_rows(k, d, high):
         below = jnp.broadcast_to(halo[k, 0, d, high : high + 1, :], (8, LANES))
         above = jnp.broadcast_to(halo[k, 1, d, high : high + 1, :], (8, LANES))
+        return below, above
+
+    def ladder_of(k, d, high, here):
+        below, above = halo_rows(k, d, high)
         lower = jnp.where(sublane == 0, below, pltpu.roll(here, 1, 0))
         upper = jnp.where(sublane == 7, above, pltpu.roll(here, 7, 0))
-        return (occ[:, cols] + constant) * (lower_weight * lower + upper_weight * upper)
+        return occupancy(d, high) * (lower_weight * lower + upper_weight * upper)
 
     def prepare(k, w_before, w):
         for copy in halo_copies(k, w):
@@ -323,13 +329,44 @@
                     value = value + fields[b] * w_before[other, pl.ds(high, 8, stride=8), :]
                 linear[rows, cols] = value
 
-    def linear_part(w_before, k, d, high):
-        value = ladder_of(k, d, high, w_before[d, pl.ds(high, 8, stride=8), :])
+    def first_step(w, inverse):
+        scale = jnp.broadcast_to(inverse, (8, LANES))
+        total = None
         for b in range(4):
-            value = value + fields[b] * w_before[d ^ (1 << b), pl.ds(high, 8, stride=8), :]
-        return value
-
-    def step(k, u_before, w_before, w, inverse, part):
+            product = flipped(jnp.dot(ub[...], a[b], preferred_element_type=F32), b)
+            total = product if total is None else total + product
+        inner_lower = jnp.where(sublane == 0, 0.0, lower_weight)
+        inner_upper = jnp.where(sublane == 7, 0.0, upper_weight)
+        for d in range(16):
+            rows = slice(d * 8, (d + 1) * 8)
+            for high in range(8):
+                cols = slice(high * 128, (high + 1) * 128)
+                here = r_in[d, pl.ds(high, 8, stride=8), :]
+                value = occupancy(d, high) * (
+                    inner_lower * pltpu.roll(here, 1, 0) + inner_upper * pltpu.roll(here, 7, 0)
+                )
+                for b in range(4):
+                    value = value + fields[b] * r_in[d ^ (1 << b), pl.ds(high, 8, stride=8), :]
+                acc[rows, cols] = total[rows, cols] + value * scale
+        for copy in halo_copies(0, r_in):
+            copy.wait_recv()
+        outer_lower = jnp.where(sublane == 0, lower_weight, 0.0) * scale
+        outer_upper = jnp.where(sublane == 7, upper_weight, 0.0) * scale
+        squares, products = zero, zero
+        for d in range(16):
+            rows = slice(d * 8, (d + 1) * 8)
+            for high in range(8):
+                cols = slice(high * 128, (high + 1) * 128)
+                below, above = halo_rows(0, d, high)
+                new = acc[rows, cols] + occupancy(d, high) * (
+                    outer_lower * below + outer_upper * above
+                )
+                w[d, pl.ds(high, 8, stride=8), :] = new
+                squares = squares + new * new
+                products = products + u_0[rows, cols] * new
+        return squares, products
+
+    def step(u_before, w, inverse, part):
         scale = jnp.broadcast_to(inverse, (8, LANES))
         total = None
         for b in range(4):
@@ -341,50 +378,17 @@
             for high in range(8):
                 cols = slice(high * 128, (high + 1) * 128)
                 new = total[rows, cols] + part(d, high) * scale
-                if k > 0:
-                    new = 2.0 * new - u_before[rows, cols] * scale
+                new = 2.0 * new - u_before[rows, cols] * scale
                 w[d, pl.ds(high, 8, stride=8), :] = new
                 squares = squares + new * new
                 products = products + u_0[rows, cols] * new
         return squares, products
 
-    def multiply():
-        total = None
-        for b in range(4):
-            product = flipped(jnp.dot(ub[...], a[b], preferred_element_type=F32), b)
-            total = product if total is None else total + product
-        acc[...] = total
-
-    def combine(k, u_before, w, inverse, send=None):
-        scale = jnp.broadcast_to(inverse, (8, LANES))
-
-        def body(i, carry):
-            squares, products = carry
-            d = (site + 1 + i) % 16
-            rows = pl.ds(pl.multiple_of(d * 8, 8), 8)
-            for high in range(8):
-                cols = slice(high * 128, (high + 1) * 128)
-                new = acc[rows, cols] + linear[rows, cols] * scale
-                if k > 0:
-                    new = 2.0 * new - u_before[rows, cols] * scale
-                w[d, pl.ds(high, 8, stride=8), :] = new
-                squares = squares + new * new
-                products = products + u_0[rows, cols] * new
-            if send is not None:
-                send(i)
-            return squares, products
-
-        return lax.fori_loop(0, 16, body, (zero, zero))
-
     def set_stat(k, value):
         stats[k] = value[0, 0]
 
     normalize(r_in, u_0, inverse)
-    for copy in halo_copies(0, r_in):
-        copy.wait_recv()
-    squares, products = step(
-        0, None, r_in, w_1, inverse, lambda d, high: linear_part(r_in, 0, d, high)
-    )
+    squares, products = first_step(w_1, inverse)
     row = jnp.where(lane < 64, fold(squares), fold(products))
     spread("whole", rows_2.at[1], slots_whole, row, send_1.at[1], recv_1.at[1])
     for copy in halo_copies(1, w_1):
@@ -395,7 +399,7 @@
 
     normalize(w_1, u_1, inverse)
     squares, products = step(
-        1, u_0, w_1, w_2, inverse,
+        u_0, w_2, inverse,
         lambda d, high: linear[d * 8 : (d + 1) * 8, high * 128 : (high + 1) * 128],
     )
     scalars_start(2, "column", squares, products)
@@ -410,7 +414,7 @@
 
     normalize(w_2, None, inverse)
     squares, products = step(
-        2, u_1, w_2, w_3, inverse,
+        u_1, w_3, inverse,
         lambda d, high: linear[d * 8 : (d + 1) * 8, high * 128 : (high + 1) * 128],
     )
     scalars_start(3, "column", squares, products)

time: 68.9 us -> 67.9 us (0.985)
  Pallas kernels: 68.1 us -> 67.2 us
    pallas_call x1, Pallas kernels: 65.9 us -> 64.9 us  [shards(): pl.pallas_call(kernel, out_shape=(block, block, jax.ShapeDtypeStruct((8,)...]
where the time goes in v8:
time: 67.9 us; the launch traced here: 67.8 us
  Pallas kernels  67.2 us (99%)
    pallas_call x1, Pallas kernels, shards(): pl.pallas_call(kernel, out_shape=(block, block, jax.ShapeDtypeStruct((8,)...  64.9 us
    pallas_call x1, Pallas kernels, shards(): pl.pallas_call(finish_kernel, out_shape=(block, block, jax.ShapeDtypeStru...  2.25 us

profile of v8, /device:TPU:1, one launch (start us, length us, event | category | flops | bytes accessed | tf_op | source)
XLA Modules:
  0.0 67.8 jit_solution(11952336334549225358)
XLA Ops:
  0.6 64.9 %shard_map.94 = (f32[1024,128]{1,0:T(8,128)}, f32[1024,128]{1,0:T(8,128)}, f32[8]{0:T(128)}) custom-call(f32[1024,128]{1,0:T(8,128)} %state.1, bf16[4,1024,1024]{2,1,0:T(8,128)(2,1)} %ops.1, s32[4,8,8]{2,1,0:T(8,128)} %mask_in.1, s32[4]{0:T(128)} %site_bits_in.1, f32[4]{0:T(128)} %field_in.1, f32[14]{0:T(128)} %site_coupling_in.1, f32[64]{0:T(128)} %mode_coupling_in.1), custom_call_target="tpu_custom_call" | custom-call | tf_op jit(solution)/shard_map/pallas_call | solution.py:488
  65.6 2.3 %shard_map.95 = (f32[1024,128]{1,0:T(8,128)}, f32[1024,128]{1,0:T(8,128)}, f32[3]{0:T(128)}) custom-call(f32[1024,128]{1,0:T(8,128)} %get-tuple-element.6.r_3, f32[1024,128]{1,0:T(8,128)} %get-tuple-element.7.ready, f32[8]{0:T(128)} %get-tuple-element.8.stats), custom_call_target="tpu_custom_call" | custom-call | tf_op jit(solution)/shard_map/pallas_call | solution.py:539

commit v9 on v8

--- a/solution.py
+++ b/solution.py
@@ -455,8 +455,8 @@
     load_2 = pltpu.make_async_copy(ready, v_2, sem.at[2])
     store = pltpu.make_async_copy(kept, moments, sem.at[3])
     store_2 = pltpu.make_async_copy(v_2, prev, sem.at[4])
+    load_3.start()
     load.start()
-    load_3.start()
     load_2.start()
     load.wait()
     for k in range(STEPS):
@@ -470,9 +470,8 @@
         out_3[rows, :] = finished(v_3, high) * scale
         stores.append(pltpu.make_async_copy(out_3.at[rows, :], last.at[rows, :], store_sem.at[high]))
         stores[high].start()
-        if high == 0:
-            load_2.wait()
-            store_2.start()
+    load_2.wait()
+    store_2.start()
     for copy in stores + [store, store_2]:
         copy.wait()
 

time: 67.9 us -> 67.9 us (level)
  no operation moved by 1% of the time
where the time goes in v9:
time: 67.9 us; the launch traced here: 67.8 us
  Pallas kernels  67.1 us (99%)
    pallas_call x1, Pallas kernels, shards(): pl.pallas_call(kernel, out_shape=(block, block, jax.ShapeDtypeStruct((8,)...  64.9 us
    pallas_call x1, Pallas kernels, shards(): pl.pallas_call(finish_kernel, out_shape=(block, block, jax.ShapeDtypeStru...  2.23 us

profile of v9, /device:TPU:1, one launch (start us, length us, event | category | flops | bytes accessed | tf_op | source)
XLA Modules:
  0.0 67.8 jit_solution(14288498810627387667)
XLA Ops:
  0.6 64.9 %shard_map.94 = (f32[1024,128]{1,0:T(8,128)}, f32[1024,128]{1,0:T(8,128)}, f32[8]{0:T(128)}) custom-call(f32[1024,128]{1,0:T(8,128)} %state.1, bf16[4,1024,1024]{2,1,0:T(8,128)(2,1)} %ops.1, s32[4,8,8]{2,1,0:T(8,128)} %mask_in.1, s32[4]{0:T(128)} %site_bits_in.1, f32[4]{0:T(128)} %field_in.1, f32[14]{0:T(128)} %site_coupling_in.1, f32[64]{0:T(128)} %mode_coupling_in.1), custom_call_target="tpu_custom_call" | custom-call | tf_op jit(solution)/shard_map/pallas_call | solution.py:487
  65.6 2.2 %shard_map.95 = (f32[1024,128]{1,0:T(8,128)}, f32[1024,128]{1,0:T(8,128)}, f32[3]{0:T(128)}) custom-call(f32[1024,128]{1,0:T(8,128)} %get-tuple-element.6.r_3, f32[1024,128]{1,0:T(8,128)} %get-tuple-element.7.ready, f32[8]{0:T(128)} %get-tuple-element.8.stats), custom_call_target="tpu_custom_call" | custom-call | tf_op jit(solution)/shard_map/pallas_call | solution.py:538
